TPU v7x, 32 devices: a whole 2x2x4 slice. The times are simulated.
32 devices in a mesh: px: 8 (over z, y), py: 4 (over x, core).
Axes of the slice: x: 2, y: 2, z: 4, core: 2. Of those that a mesh axis runs over, the one named last changes fastest.
Arguments:
- field: bfloat16 [2, 64, 64, 4096], P(None, 'px', 'py'), may hold values from -6 to 6
- cotangent: bfloat16 [2, 64, 64, 4096], P(None, 'px', 'py'), may hold values from -6 to 6
- taps: bfloat16 [3, 64, 64, 64], replicated, may hold values from -1 to 1.5, as said below
Outputs:
- mapped: bfloat16 [2, 64, 64, 4096], P(None, 'px', 'py')
- grad_field: bfloat16 [2, 64, 64, 4096], P(None, 'px', 'py')
- grad_taps: float32 [3, 64, 64, 64], P(None, 'px', 'py')
Inputs may be any that keep to these rules, and one draw needn't show every extreme that they name: Every diagonal entry taps[a, 0, c, c] lies between 1 and 1.5, and every diagonal entry taps[a, t, c, c] with t >= 1 has magnitude at most 0.4 / 64.
All inputs are finite; a program needn't handle non-finite values.
Results may differ from a plain program's by a relative error of at most 0.018.
Values may be sent and summed in bfloat16 or wider, within the bound.
No kernel may reach another device: no remote copies, remote signals or barrier semaphores. Data moves between devices by JAX's collectives and lax.ppermute only.
A program may use at most 192 MiB of HBM per device.

v0:
```python
import math

import jax
import jax.numpy as jnp
from jax import lax
from jax.sharding import PartitionSpec as P

N = 64
C = 64


def dft_tables(row_ids, col_ids, length):
    product = row_ids[:, None] * col_ids[None, :] % length
    angle = product.astype(jnp.float32) * (2.0 * math.pi / length)
    return (jnp.cos(angle), jnp.sin(angle))


def along(values, table, position):
    letters = "abcdef"[: values.ndim]
    target = letters[:position] + "k" + letters[position + 1 :]
    return jnp.einsum(
        letters + ",k" + letters[position] + "->" + target,
        values,
        table,
        preferred_element_type=jnp.float32,
    )


def section(values, position, cos_b, sin_b, turn_sign, factor):
    direct = along(values, cos_b, position)
    crossed = along(values, sin_b, position)
    half = values.shape[-1] // 2
    turned = jnp.concatenate([crossed[..., half:], -crossed[..., :half]], -1)
    return ((direct + turn_sign * turned) * factor).astype(jnp.bfloat16)


def z_forward(values, cos_b, sin_b):
    direct = along(values, cos_b, 3)
    crossed = along(values, sin_b, 3)
    return jnp.concatenate([direct, -crossed], -1).astype(jnp.bfloat16)


def z_inverse(values, cos_b, sin_b, factor):
    half = values.shape[-1] // 2
    real_part = along(values[..., :half], cos_b, 3)
    imag_part = along(values[..., half:], sin_b, 3)
    return ((real_part - imag_part) * factor).astype(jnp.bfloat16)


def spectra(taps_axis, cos_b, sin_b):
    real_w = jnp.einsum("kt,toi->koi", cos_b, taps_axis, preferred_element_type=jnp.float32)
    imag_w = -jnp.einsum("kt,toi->koi", sin_b, taps_axis, preferred_element_type=jnp.float32)
    upper = jnp.concatenate([real_w, -imag_w], 2)
    lower = jnp.concatenate([imag_w, real_w], 2)
    return jnp.concatenate([upper, lower], 1).astype(jnp.bfloat16)


def push(values, matrix, position):
    letters = "abcde"
    return jnp.einsum(
        letters + "," + letters[position] + "fe->abcdf",
        values,
        matrix,
        preferred_element_type=jnp.float32,
    ).astype(jnp.bfloat16)


def pull(values, matrix, position):
    letters = "abcde"
    return jnp.einsum(
        letters + "," + letters[position] + "ef->abcdf",
        values,
        matrix,
        preferred_element_type=jnp.float32,
    ).astype(jnp.bfloat16)


def outer(left, right, position):
    letters = "abcde"
    return jnp.einsum(
        "abcde,abcdf->" + letters[position] + "ef", left, right, preferred_element_type=jnp.float32
    )


def tap_terms(spectral, cos_f, sin_f, split_t, split_o):
    width = spectral.shape[1] // 2
    count = spectral.shape[0]
    real_g = spectral[:, :width, :width] + spectral[:, width:, width:]
    imag_g = spectral[:, :width, width:] - spectral[:, width:, :width]
    cos_r = cos_f.reshape(count, split_t, -1)
    sin_r = sin_f.reshape(count, split_t, -1)
    real_r = real_g.reshape(count, split_o, -1, width)
    imag_r = imag_g.reshape(count, split_o, -1, width)
    highest = lax.Precision.HIGHEST
    return jnp.einsum("kpu,kqvi->pquvi", cos_r, real_r, precision=highest) + jnp.einsum(
        "kpu,kqvi->pquvi", sin_r, imag_r, precision=highest
    )


def log_terms(taps, row_ids, col_ids, length):
    highest = lax.Precision.HIGHEST
    diag_w = jnp.diagonal(taps.astype(jnp.float32), axis1=2, axis2=3)
    cos_full, sin_full = dft_tables(row_ids, row_ids, length)
    real_z = jnp.einsum("kt,atc->akc", cos_full, diag_w, precision=highest)
    imag_z = -jnp.einsum("kt,atc->akc", sin_full, diag_w, precision=highest)
    modulus = real_z * real_z + imag_z * imag_z
    cos_cols, sin_cols = dft_tables(row_ids, col_ids, length)
    summed = jnp.einsum("kt,akc->atc", cos_cols, real_z / modulus, precision=highest) - jnp.einsum(
        "kt,akc->atc", sin_cols, imag_z / modulus, precision=highest
    )
    return summed / math.sqrt(length)


def per_device(field, cotangent, taps):
    batch_rows = field.shape[0]
    local_x = field.shape[1]
    local_y = field.shape[2]
    count_px = lax.axis_size("px")
    count_py = lax.axis_size("py")
    all_ids = jnp.arange(N, dtype=jnp.int32)
    cos_f, sin_f = dft_tables(all_ids, all_ids, N)
    cos_b = cos_f.astype(jnp.bfloat16)
    sin_b = sin_f.astype(jnp.bfloat16)
    stacked = jnp.concatenate([field, cotangent], 0).reshape(2 * batch_rows, local_x, local_y, N, C)
    spectral = z_forward(stacked, cos_b, sin_b)
    spectral = section(
        lax.all_to_all(spectral, "py", split_axis=3, concat_axis=2, tiled=True),
        2,
        cos_b,
        sin_b,
        1.0,
        1.0,
    )
    spectral = section(
        lax.all_to_all(spectral, "px", split_axis=2, concat_axis=1, tiled=True),
        1,
        cos_b,
        sin_b,
        1.0,
        1.0,
    )
    field_hat = spectral[:batch_rows]
    cot_hat = spectral[batch_rows:]
    count_ky = N // count_px
    count_kz = N // count_py
    ky_ids = lax.axis_index("px") * count_ky + jnp.arange(count_ky, dtype=jnp.int32)
    kz_ids = lax.axis_index("py") * count_kz + jnp.arange(count_kz, dtype=jnp.int32)
    cos_y, sin_y = dft_tables(ky_ids, all_ids, N)
    cos_z, sin_z = dft_tables(kz_ids, all_ids, N)
    lower_mask = jnp.tril(jnp.ones((C, C), jnp.float32))
    masked = (taps.astype(jnp.float32) * lower_mask).astype(jnp.bfloat16)
    mix_x = spectra(masked[0], cos_b, sin_b)
    mix_y = spectra(masked[1], cos_y.astype(jnp.bfloat16), sin_y.astype(jnp.bfloat16))
    mix_z = spectra(masked[2], cos_z.astype(jnp.bfloat16), sin_z.astype(jnp.bfloat16))
    first = push(field_hat, mix_z, 3)
    second = push(first, mix_y, 2)
    out_hat = push(second, mix_x, 1)
    back_two = pull(cot_hat, mix_x, 1)
    back_one = pull(back_two, mix_y, 2)
    back_hat = pull(back_one, mix_z, 3)
    grad_x_spec = outer(cot_hat, second, 1)
    grad_y_spec = outer(back_two, first, 2)
    grad_z_spec = outer(back_one, field_hat, 3)
    returned = section(jnp.concatenate([out_hat, back_hat], 0), 1, cos_b, sin_b, -1.0, 1.0 / N)
    returned = section(
        lax.all_to_all(returned, "px", split_axis=1, concat_axis=2, tiled=True),
        2,
        cos_b,
        sin_b,
        -1.0,
        1.0 / N,
    )
    returned = z_inverse(
        lax.all_to_all(returned, "py", split_axis=2, concat_axis=3, tiled=True),
        cos_b,
        sin_b,
        1.0 / N,
    )
    returned = returned.reshape(2 * batch_rows, local_x, local_y, N * C)
    mapped = returned[:batch_rows]
    grad_field = returned[batch_rows:]
    data_scale = 1.0 / (float(N) ** 4 * math.sqrt(N))
    slab_t = N // count_px
    slab_o = C // count_py
    t_ids = lax.axis_index("px") * slab_t + jnp.arange(slab_t, dtype=jnp.int32)
    o_ids = lax.axis_index("py") * slab_o + jnp.arange(slab_o, dtype=jnp.int32)
    terms = (
        jnp.stack(
            [
                tap_terms(grad_x_spec, cos_f, sin_f, 1, 1),
                tap_terms(grad_y_spec, cos_y, sin_y, 1, 1),
                tap_terms(grad_z_spec, cos_z, sin_z, 1, 1),
            ],
            2,
        )
        * data_scale
    ).reshape(3, N, C, C)
    summed = lax.psum_scatter(
        terms.astype(jnp.bfloat16), "px", scatter_dimension=1, tiled=True
    ).astype(jnp.float32)
    summed = lax.psum_scatter(
        summed.astype(jnp.bfloat16), "py", scatter_dimension=2, tiled=True
    ).astype(jnp.float32)
    log_part = log_terms(taps, all_ids, t_ids, N)
    channel_ids = jnp.arange(C, dtype=jnp.int32)
    diagonal_sel = (channel_ids[None, :] == o_ids[:, None]).astype(jnp.float32)
    keep_mask = (channel_ids[None, :] <= o_ids[:, None]).astype(jnp.float32)
    grad_taps = keep_mask * (summed - log_part[:, :, None, :] * diagonal_sel)
    return (mapped, grad_field, grad_taps)


def solution(mesh):
    return jax.shard_map(
        per_device,
        mesh=mesh,
        in_specs=(P(None, "px", "py", None), P(None, "px", "py", None), P()),
        out_specs=(P(None, "px", "py", None), P(None, "px", "py", None), P(None, "px", "py", None)),
        check_vma=False,
    )
```

profile of v0, /device:TPU:0, one launch (start us, length us, event | category | flops | bytes accessed | tf_op | source)
XLA Modules:
  0.0 974.7 jit_solution(12019868049282666436)
XLA Ops:
  7.2 4.6 pad_maximum_fusion.2
  11.7 12.6 %reshape.274 = bf16[4,8,16,64,64]{4,3,2,1,0:T(8,128)(2,1)} reshape(bf16[4,8,16,4096]{3,2,1,0:T(8,128)(2,1)} %pad_maximum_fusion.2) | data formatting | bytes 8388608 | tf_op jit(solution)/shard_map/reshape | solution.py:124
  24.4 6.0 convert_bitcast_fusion
  30.3 5.7 fusion.22
  36.0 9.5 pad_maximum_fusion
  45.5 12.0 %copy.82 = bf16[4,8,16,64,128]{4,2,1,0,3:T(8,128)(2,1)} copy(bf16[4,8,16,64,128]{4,3,2,1,0:T(8,128)(2,1)} %pad_maximum_fusion) | data formatting | bytes 16777216 | tf_op jit(solution)/shard_map/concatenate | solution.py:40
  57.5 101.5 %all_to_all.72 = bf16[4,8,16,64,128]{4,2,1,0,3:T(8,128)(2,1)} all-to-all(bf16[4,8,16,64,128]{4,2,1,0,3:T(8,128)(2,1)} %copy.82), channel_id=1, replica_groups=mesh['px'=8,'py'=4] {'py'}, dimensions={3} | all-to-all | bytes 16777216 | tf_op jit(solution)/shard_map/all_to_all | solution.py:127
  159.0 9.1 copy.83
  168.1 5.8 convolution_bitcast_fusion.3
  174.0 12.3 %fusion.313 = (f32[4,8,64,16,64]{4,2,3,1,0:T(8,128)}, f32[4,8,64,16,64]{4,2,3,1,0:T(8,128)}) fusion(f32[4,8,64,16,128]{4,2,3,1,0:T(8,128)S(1)} %convolution_bitcast_fusion.3), kind=kLoop, calls=%fused_computation.331 | loop fusion | flops 2097152 | bytes 33554432 | tf_op jit(solution)/shard_map/slice | solution.py:33
  186.3 19.4 %fusion = bf16[4,8,64,16,128]{4,2,3,1,0:T(8,128)(2,1)} fusion(f32[4,8,64,16,64]{4,2,3,1,0:T(8,128)} %get-tuple-element.19, f32[4,8,64,16,64]{4,2,3,1,0:T(8,128)} %get-tuple-element.18, bf16[4,8,64,16,128]{4,2,3,1,0:T(8,128)(2,1)} %bitcast.229), kind=kOutput, calls=%fused_computation.6 | convolution fusion | flops 549515264 | bytes 33554432 | tf_op jit(solution)/shard_map/abcde,kc->abkde/dot_general | solution.py:21
  205.7 12.1 %copy.84 = bf16[4,8,64,16,128]{4,3,1,0,2:T(8,128)(2,1)} copy(bf16[4,8,64,16,128]{4,2,3,1,0:T(8,128)(2,1)} %fusion) | data formatting | bytes 16777216 | tf_op jit(solution)/shard_map/convert_element_type | solution.py:34
  217.8 7.1 all-to-all-start.1
  231.3 176.3 %all-to-all-done.1 = bf16[4,8,64,16,128]{4,3,1,0,2:T(8,128)(2,1)} async-done(((bf16[4,8,64,16,128]{4,3,1,0,2:T(8,128)(2,1)}), bf16[4,8,64,16,128]{4,3,1,0,2:T(8,128)(2,1)}, u32[]{:S(2)}, u32[]{:S(2)}) %all-to-all-start.1) | async-done | bytes 8388640 | tf_op jit(solution)/shard_map/all_to_all | solution.py:135
  407.6 5.8 convolution_bitcast_fusion.2
  413.4 12.3 %fusion.312 = (f32[4,64,8,16,64]{4,1,3,2,0:T(8,128)}, f32[4,64,8,16,64]{4,1,3,2,0:T(8,128)}) fusion(f32[4,64,8,16,128]{4,1,3,2,0:T(8,128)S(1)} %convolution_bitcast_fusion.2), kind=kLoop, calls=%fused_computation.330 | loop fusion | flops 2097152 | bytes 33554432 | tf_op jit(solution)/shard_map/slice | solution.py:33
  425.8 19.1 %fusion.1 = bf16[4,64,8,16,128]{4,1,3,2,0:T(8,128)(2,1)} fusion(f32[4,64,8,16,64]{4,1,3,2,0:T(8,128)} %get-tuple-element.17, f32[4,64,8,16,64]{4,1,3,2,0:T(8,128)} %get-tuple-element.16, bf16[4,8,8,8,16,128]{5,4,1,0,3,2:T(8,128)(2,1)} %bitcast.26), kind=kOutput, calls=%fused_computation.8 | convolution fusion | flops 549515264 | bytes 33554432 | tf_op jit(solution)/shard_map/abcde,kb->akcde/dot_general | solution.py:21
  444.9 4.9 fusion.315
  454.3 4.3 convert_bitcast_fusion.2
  466.7 4.9 copy.245
  471.6 6.4 convert_bitcast_fusion.3
  478.0 7.4 pad_maximum_fusion.1
  485.4 10.3 %convolution_bitcast_fusion.1 = f32[4,64,8,16,128]{4,1,3,2,0:T(8,128)S(1)} fusion(bf16[4,64,8,16,128]{4,3,2,0,1:T(8,128)(2,1)} %pad_maximum_fusion.1), kind=kOutput, calls=%fused_computation.20 | convolution fusion | flops 536932352 | bytes 25165824 | tf_op jit(solution)/shard_map/abcde,kb->akcde/dot_general | solution.py:21
  495.8 12.3 %fusion.311 = (f32[4,64,8,16,64]{4,1,3,2,0:T(8,128)}, f32[4,64,8,16,64]{4,1,3,2,0:T(8,128)}) fusion(f32[4,64,8,16,128]{4,1,3,2,0:T(8,128)S(1)} %convolution_bitcast_fusion.1), kind=kLoop, calls=%fused_computation.329 | loop fusion | flops 2097152 | bytes 33554432 | tf_op jit(solution)/shard_map/slice | solution.py:33
  508.1 20.7 %fusion.4 = bf16[4,64,8,16,128]{4,1,3,2,0:T(8,128)(2,1)} fusion(f32[4,64,8,16,64]{4,1,3,2,0:T(8,128)} %get-tuple-element.15, f32[4,64,8,16,64]{4,1,3,2,0:T(8,128)} %get-tuple-element.14, bf16[4,64,8,16,128]{4,3,2,0,1:T(8,128)(2,1)} %pad_maximum_fusion.1), kind=kOutput, calls=%fused_computation.12 | convolution fusion | flops 557903872 | bytes 33554432 | tf_op jit(solution)/shard_map/abcde,kb->akcde/dot_general | solution.py:21
  528.8 12.0 %copy.101 = bf16[4,64,8,16,128]{4,3,2,0,1:T(8,128)(2,1)} copy(bf16[4,64,8,16,128]{4,1,3,2,0:T(8,128)(2,1)} %fusion.4) | data formatting | bytes 16777216 | tf_op jit(solution)/shard_map/convert_element_type | solution.py:34
  540.8 5.1 all-to-all-start.2
  546.0 4.8 fusion.70
  554.6 4.8 add_bitcast_fusion
  566.6 161.3 %all-to-all-done.2 = bf16[4,64,8,16,128]{4,3,2,0,1:T(8,128)(2,1)} async-done(((bf16[4,64,8,16,128]{4,3,2,0,1:T(8,128)(2,1)}), bf16[4,64,8,16,128]{4,3,2,0,1:T(8,128)(2,1)}, u32[]{:S(2)}, u32[]{:S(2)}) %all-to-all-start.2) | async-done | bytes 8388640 | tf_op jit(solution)/shard_map/all_to_all | solution.py:166
  727.8 5.8 convolution_bitcast_fusion
  733.7 12.3 %fusion.310 = (f32[4,8,64,16,64]{4,2,3,1,0:T(8,128)}, f32[4,8,64,16,64]{4,2,3,1,0:T(8,128)}) fusion(f32[4,8,64,16,128]{4,2,3,1,0:T(8,128)S(1)} %convolution_bitcast_fusion), kind=kLoop, calls=%fused_computation.328 | loop fusion | flops 2097152 | bytes 33554432 | tf_op jit(solution)/shard_map/slice | solution.py:33
  746.0 19.6 %fusion.7 = bf16[4,8,64,16,128]{4,2,3,1,0:T(8,128)(2,1)} fusion(f32[4,8,64,16,64]{4,2,3,1,0:T(8,128)} %get-tuple-element.13, f32[4,8,64,16,64]{4,2,3,1,0:T(8,128)} %get-tuple-element.12, bf16[4,8,8,8,16,128]{5,4,3,0,2,1:T(8,128)(2,1)} %bitcast.43), kind=kOutput, calls=%fused_computation.16 | convolution fusion | flops 557903872 | bytes 33554432 | tf_op jit(solution)/shard_map/abcde,kc->abkde/dot_general | solution.py:21
  765.6 12.0 %copy.103 = bf16[4,8,64,16,128]{4,3,1,0,2:T(8,128)(2,1)} copy(bf16[4,8,64,16,128]{4,2,3,1,0:T(8,128)(2,1)} %fusion.7) | data formatting | bytes 16777216 | tf_op jit(solution)/shard_map/convert_element_type | solution.py:34
  777.6 5.7 all-to-all-start.3
  787.0 8.8 fusion.57
  796.9 4.6 fusion.62
  801.5 4.4 add_bitcast_fusion.2
  808.1 5.5 copy.116
  814.0 5.5 copy.118
  823.7 64.1 %reduce-scatter.3.cloned.1.call-done = bf16[3,8,64,64]{3,2,0,1:T(8,128)(2,1)} async-done(((bf16[3,64,64,64]{3,2,0,1:T(8,128)(2,1)}), bf16[3,8,64,64]{3,2,0,1:T(8,128)(2,1)}) %reduce-scatter.3.cloned.1.call-update) | async-done | bytes 196624 | tf_op jit(solution)/shard_map/reduce_scatter | solution.py:198
  890.3 20.5 %reduce-scatter.5.cloned.1.call-done = bf16[3,8,16,64]{3,1,0,2:T(8,128)(2,1)} async-done(((bf16[3,8,64,64]{3,1,0,2:T(8,128)(2,1)}), bf16[3,8,16,64]{3,1,0,2:T(8,128)(2,1)}) %reduce-scatter.5.cloned.1.call-update) | async-done | bytes 49168 | tf_op jit(solution)/shard_map/reduce_scatter | solution.py:201
  912.4 9.1 copy.104
  921.5 11.5 %fusion.9 = f32[64,4,8,16,64]{4,0,3,2,1:T(8,128)} fusion(bf16[4,8,16,64,128]{4,3,2,1,0:T(8,128)(2,1)} %bitcast.226), kind=kOutput, calls=%fused_computation.24 | convolution fusion | flops 268496896 | bytes 16777216 | tf_op jit(solution)/shard_map/abcde,kd->abcke/dot_general | solution.py:21
  933.1 14.2 %fusion.23 = bf16[4,8,16,64,64]{4,3,2,1,0:T(8,128)(2,1)} fusion(f32[64,4,8,16,64]{4,0,3,2,1:T(8,128)} %fusion.9, bf16[4,8,16,64,128]{4,3,2,1,0:T(8,128)(2,1)} %bitcast.227), kind=kOutput, calls=%fused_computation.44 | convolution fusion | flops 274788352 | bytes 20971520 | tf_op jit(solution)/shard_map/abcde,kd->abcke/dot_general | solution.py:21
  947.3 6.9 fusion.314
  954.2 6.6 slice.109
  960.8 6.6 slice.111
  (62 shorter events, 45.4 us)
Async XLA Ops:
  24.4 6.0 copy-start
  217.8 7.1 copy-start.5
  217.8 189.8 %all-to-all-start.1 = ((bf16[4,8,64,16,128]{4,3,1,0,2:T(8,128)(2,1)}), bf16[4,8,64,16,128]{4,3,1,0,2:T(8,128)(2,1)}, u32[]{:S(2)}, u32[]{:S(2)}) async-start(bf16[4,8,64,16,128]{4,3,1,0,2:T(8,128)(2,1)} %copy.84), calls=%async_computation.1 | async-start | bytes 16777216 | tf_op jit(solution)/shard_map/all_to_all | solution.py:135
  449.7 4.5 copy-start.10
  451.0 2.0 copy-start.2
  454.3 17.4 %copy-start.1 = (bf16[2,64,8,16,128]{4,1,3,0,2:T(8,128)(2,1)}, bf16[2,64,8,16,128]{4,1,3,0,2:T(8,128)(2,1)S(1)}, u32[]{:S(2)}) copy-start(bf16[2,64,8,16,128]{4,1,3,0,2:T(8,128)(2,1)S(1)} %convert_bitcast_fusion.4) | copy-start | bytes 12582916
  458.6 2.0 copy-start.8
  463.5 2.0 copy-start.4
  540.8 187.0 %all-to-all-start.2 = ((bf16[4,64,8,16,128]{4,3,2,0,1:T(8,128)(2,1)}), bf16[4,64,8,16,128]{4,3,2,0,1:T(8,128)(2,1)}, u32[]{:S(2)}, u32[]{:S(2)}) async-start(bf16[4,64,8,16,128]{4,3,2,0,1:T(8,128)(2,1)} %copy.101), calls=%async_computation.2 | async-start | bytes 16777216 | tf_op jit(solution)/shard_map/all_to_all | solution.py:166
  550.8 8.6 copy-start.3
  550.8 8.6 copy-start.9
  777.6 134.8 %all-to-all-start.3 = ((bf16[4,8,64,16,128]{4,3,1,0,2:T(8,128)(2,1)}), bf16[4,8,64,16,128]{4,3,1,0,2:T(8,128)(2,1)}, u32[]{:S(2)}, u32[]{:S(2)}) async-start(bf16[4,8,64,16,128]{4,3,1,0,2:T(8,128)(2,1)} %copy.103), calls=%async_computation.3 | async-start | bytes 16777216 | tf_op jit(solution)/shard_map/all_to_all | solution.py:174
  783.3 104.5 %reduce-scatter.3.cloned.1.call-start = ((), (), s32[]{:S(2)}) async-start(), calls=%async_computation.6 | async-start | bytes 3538944 | tf_op jit(solution)/shard_map/reduce_scatter | solution.py:198
  796.9 9.1 copy-start.7
  808.1 5.8 copy-start.6
  813.7 97.1 %reduce-scatter.5.cloned.1.call-start = ((), (), s32[]{:S(2)}) async-start(), calls=%async_computation.7 | async-start | bytes 491520 | tf_op jit(solution)/shard_map/reduce_scatter | solution.py:201
Sparse Core Ops, SparseCore 0:
  813.8 73.9 reduce-scatter.2
  890.8 19.9 reduce-scatter.4
where the time goes:
time: 982 us; the launch traced here: 975 us
  waiting for transfers between devices  422 us (43%)
  matrix products  206 us (21%)
  local copies, waits for them, and re-layouts  132 us (13%)
  blocking collectives  101 us (10%)
  other arithmetic  79.9 us (8%)
  starting transfers between devices  18.4 us (2%)
  between operations  14.9 us (2%)
    all_to_all x1, waiting for transfers between devices, per_device(): lax.all_to_all(spectral, 'px', split_axis=2, concat_axis=1, tiled=True)  176 us
    all_to_all x1, waiting for transfers between devices, per_device(): lax.all_to_all(returned, 'px', split_axis=1, concat_axis=2, tiled=True)  161 us
    dot_general x12, matrix products, along(): jnp.einsum(letters + ',k' + letters[position] + '->' + target, values, ta...  144 us
    all_to_all x1, blocking collectives, per_device(): lax.all_to_all(spectral, 'py', split_axis=3, concat_axis=2, tiled=True)  101 us
    reduce_scatter x1, waiting for transfers between devices, per_device(): lax.psum_scatter(terms.astype(jnp.bfloat16), 'px', scatter_dimension=1, t...  64.1 us
    slice x4, other arithmetic, section(): turned = jnp.concatenate([crossed[..., half:], -crossed[..., :half]], -1)  49.4 us
    convert_element_type x3, local copies, waits for them, and re-layouts, section(): return ((direct + turn_sign * turned) * factor).astype(jnp.bfloat16)  36.1 us
    reduce_scatter x1, waiting for transfers between devices, per_device(): lax.psum_scatter(summed.astype(jnp.bfloat16), 'py', scatter_dimension=2,...  20.5 us
  transfers between devices with their start and end apart: 5, of which 4 were waited for; matrix products, arithmetic and copies ran while one was open for 7% of the time, Pallas kernels for 0%

commit v1 on v0

--- a/solution.py
+++ b/solution.py
@@ -2,17 +2,553 @@
 
 import jax
 import jax.numpy as jnp
+import numpy as np
 from jax import lax
+from jax.experimental import pallas as pl
+from jax.experimental.pallas import tpu as pltpu
 from jax.sharding import PartitionSpec as P
 
 N = 64
 C = 64
+F32 = jnp.float32
+BF16 = jnp.bfloat16
+
+
+def real_dft(length):
+    half = length // 2
+    slot = np.arange(half)[:, None]
+    at = np.arange(length)[None, :]
+    angle = 2.0 * np.pi * ((slot * at) % length) / length
+    real = np.cos(angle)
+    imag = -np.sin(angle)
+    imag[0] = (-1.0) ** np.arange(length)
+    forward = np.concatenate([real, imag], 0)
+    weight = np.where(np.arange(half) == 0, 1.0, 2.0) / length
+    inverse = (forward * np.concatenate([weight, weight])[:, None]).T
+    return forward, inverse
+
+
+def line_table():
+    at = np.arange(N)[None, :]
+    freq = np.arange(N // 2 + 1)[:, None]
+    angle = 2.0 * np.pi * ((freq * at) % N) / N
+    return np.concatenate([np.cos(angle), -np.sin(angle[: N // 2]), np.zeros((7, N))], 0)
+
+
+def pair_table():
+    length = N // 2
+    half = length // 2
+    slot = np.arange(half)
+    table = np.zeros((2, 2, 2, half, 2, N))
+    for row in range(2):
+        for col in range(2):
+            for t in range((row + col) % 2, N, 2):
+                lag = (t - col + row) // 2
+                angle = 2.0 * np.pi * ((slot * lag) % length) / length
+                cos, sin = np.cos(angle), np.sin(angle)
+                other = cos.copy()
+                other[0] = (-1.0) ** lag
+                sin[0] = 0.0
+                table[col, 0, 0, :, row, t] = cos
+                table[col, 1, 1, :, row, t] = other
+                table[col, 0, 1, :, row, t] = -sin
+                table[col, 1, 0, :, row, t] = sin
+    return table.reshape(8 * half, 2 * N)
+
+
+def lag_rows(length, lag):
+    half = length // 2
+    slot = np.arange(half)
+    angle = 2.0 * np.pi * ((slot * lag) % length) / length
+    weight = np.where(slot == 0, 1.0, 2.0) / length
+    real = np.cos(angle) * weight
+    imag = np.sin(angle) * weight
+    imag[0] = (-1.0) ** lag / length
+    return np.concatenate([real, imag])
+
+
+def tap_tables():
+    scale = float(N) ** -1.5
+    half = N // 2
+    direct = np.stack([lag_rows(N, t) for t in range(N)], 0)
+    paired = np.stack([np.concatenate([lag_rows(half, d), lag_rows(half, d + 1)]) for d in range(half)], 0)
+    return direct * scale, paired * scale
+
+
+def dot(a, b):
+    return jnp.dot(a, b, preferred_element_type=F32)
+
+
+def dot_nt(a, b):
+    return lax.dot_general(a, b, (((1,), (1,)), ((), ())), preferred_element_type=F32)
+
+
+def dot_tn(a, b):
+    return lax.dot_general(a, b, (((0,), (0,)), ((), ())), preferred_element_type=F32)
+
+
+def whole(count):
+    return [pl.BlockSpec(memory_space=pltpu.VMEM)] * count
+
+
+def params(megabytes):
+    return pltpu.CompilerParams(vmem_limit_bytes=megabytes << 20)
+
+
+def expand_to(out_ref, table_ref, row_of, col_of, row_lane, col_lane):
+    size = out_ref.shape[0]
+    small_rows, small_cols = table_ref.shape
+    pick = lax.broadcasted_iota(jnp.int32, (small_cols, size), 0)
+    wide = lax.broadcasted_iota(jnp.int32, (small_cols, size), 1)
+    columns = jnp.where(pick == col_of(wide), 1.0, 0.0).astype(BF16)
+    chunk = 256
+
+    @pl.loop(0, size // chunk)
+    def _(step):
+        base = step * chunk
+        tall = lax.broadcasted_iota(jnp.int32, (chunk, small_rows), 0) + base
+        which = lax.broadcasted_iota(jnp.int32, (chunk, small_rows), 1)
+        rows = jnp.where(row_of(tall) == which, 1.0, 0.0).astype(BF16)
+        values = dot(dot(rows, table_ref[...]).astype(BF16), columns)
+        at_row = lax.broadcasted_iota(jnp.int32, (chunk, size), 0) + base
+        at_col = lax.broadcasted_iota(jnp.int32, (chunk, size), 1)
+        keep = row_lane(at_row) == col_lane(at_col)
+        out_ref[pl.ds(pl.multiple_of(base, chunk), chunk), :] = jnp.where(keep, values, 0.0).astype(BF16)
+
+
+def high(v):
+    return v // 16
+
+
+def low(v):
+    return v % 16
+
+
+def y_position(v):
+    return (v // 256) * 16 + v % 16
+
+
+def y_lane(v):
+    return (v // 16) % 16
+
+
+def tables_kernel(fwd, inv, fwd_z, inv_z, fx, ix, fy, iy, fz, iz):
+    expand_to(fz, fwd_z, high, high, low, low)
+    expand_to(iz, inv_z, high, high, low, low)
+    expand_to(fx, fwd, high, high, low, low)
+    expand_to(ix, inv, high, high, low, low)
+    expand_to(fy, fwd, high, y_position, low, y_lane)
+    expand_to(iy, inv, y_position, high, y_lane, low)
+
+
+def tables(fwd, inv, fwd_z, inv_z):
+    big = jax.ShapeDtypeStruct((1024, 1024), BF16)
+    small = jax.ShapeDtypeStruct((512, 512), BF16)
+    return pl.pallas_call(
+        tables_kernel,
+        out_shape=(big, big, big, big, small, small),
+        in_specs=whole(4),
+        out_specs=tuple(whole(6)),
+        compiler_params=params(40),
+        cost_estimate=pl.CostEstimate(flops=2 << 30, bytes_accessed=12 << 20, transcendentals=0),
+        name="tables",
+    )(fwd, inv, fwd_z, inv_z)
+
+
+def mixing_kernel(taps, e_line, e_pair, mix_x, mix_y, mix_z, wide, lines, pairs):
+    row = lax.broadcasted_iota(jnp.int32, (64, 64, 64), 1)
+    col = lax.broadcasted_iota(jnp.int32, (64, 64, 64), 2)
+    for axis in range(3):
+        masked = jnp.where(col <= row, taps[axis].astype(F32), 0.0).reshape(4096, 64)
+        wide[:, :64] = masked
+        wide[:, 64:] = jnp.zeros_like(masked)
+
+        if axis < 2:
+            out = mix_x if axis == 0 else mix_y
+
+            @pl.loop(0, 64, unroll=8)
+            def _(co):
+                at = wide[pl.ds(co, 64, stride=64), :].astype(BF16)
+                lines[pl.ds(co, 72, stride=64), :] = dot(e_line[...], at)
+
+            @pl.loop(0, 32, unroll=4)
+            def _(slot):
+                def block(index):
+                    one = lines[pl.ds(pl.multiple_of(index * 64, 64), 64), :]
+                    return jnp.concatenate([one, pltpu.roll(one, 64, 1)], 0)
+
+                imag = block(33 + slot)
+                out[0, 0, slot] = block(slot).astype(BF16)
+                out[1, 1, slot] = block(jnp.where(slot == 0, 32, slot)).astype(BF16)
+                out[1, 0, slot] = imag.astype(BF16)
+                out[0, 1, slot] = (-imag).astype(BF16)
+
+        else:
+
+            @pl.loop(0, 64, unroll=8)
+            def _(co):
+                at = wide[pl.ds(co, 64, stride=64), :]
+                both = jnp.concatenate([at, pltpu.roll(at, 64, 1)], 0).astype(BF16)
+                got = dot(e_pair[...], both)
+                pairs[pl.ds(co, 64, stride=128), :] = got[:64]
+                pairs[pl.ds(co + 64, 64, stride=128), :] = got[64:]
+
+            for ri in range(2):
+                for to in range(2):
+
+                    @pl.loop(0, 16, unroll=4)
+                    def _(slot):
+                        start = ((ri * 2 + to) * 16 + slot) * 128
+                        mix_z[to, ri, slot] = pairs[pl.ds(pl.multiple_of(start, 128), 128), :].astype(BF16)
+
+
+def mixing(taps, e_line, e_pair):
+    line = jax.ShapeDtypeStruct((2, 2, 32, 128, 128), BF16)
+    pair = jax.ShapeDtypeStruct((2, 2, 16, 128, 128), BF16)
+    return pl.pallas_call(
+        mixing_kernel,
+        out_shape=(line, line, pair),
+        in_specs=whole(3),
+        out_specs=tuple(whole(3)),
+        scratch_shapes=[
+            pltpu.VMEM((4096, 128), F32),
+            pltpu.VMEM((72 * 64, 128), F32),
+            pltpu.VMEM((64 * 128, 128), F32),
+        ],
+        compiler_params=params(40),
+        cost_estimate=pl.CostEstimate(flops=2 << 30, bytes_accessed=12 << 20, transcendentals=0),
+        name="mixing",
+    )(taps, e_line, e_pair)
+
+
+def mix_matrix(mix_ref, slot):
+    top = jnp.concatenate([mix_ref[0, 0, slot], mix_ref[0, 1, slot]], 1)
+    bottom = jnp.concatenate([mix_ref[1, 0, slot], mix_ref[1, 1, slot]], 1)
+    return jnp.concatenate([top, bottom], 0)
+
+
+def mix_apply(val, matrix, adjoint):
+    return (dot(val, matrix) if adjoint else dot_nt(val, matrix)).astype(BF16)
+
+
+def gradient_blocks(cot, val, slot):
+    outer = dot_tn(cot, val)
+    first = slot == 0
+    real_real = outer[:128, :128]
+    imag_imag = outer[128:, 128:]
+    crossed = outer[:128, 128:] - outer[128:, :128]
+    real = jnp.where(first, real_real, real_real + imag_imag)
+    imag = jnp.where(first, imag_imag, crossed)
+    return real, imag
+
+
+def to_lags(table, sums, out):
+    lags, depth = table.shape
+
+    @pl.loop(0, 64, unroll=8)
+    def _(co):
+        rows = sums[pl.ds(co, depth, stride=64), :]
+        out[pl.ds(co, lags, stride=64), :] = jnp.dot(
+            table[...], rows, preferred_element_type=F32, precision=lax.Precision.HIGHEST
+        )
+
+
+def line_pass(axis, adjoint, values, fwd, inv, mix, out, spec, mixed, rhs, accumulate=None):
+    @pl.loop(0, 4)
+    def _(j):
+        for h in range(2):
+            block = values[:, j, h] if axis == "x" else values[2 * j + h]
+            rhs[:, h * 128 : (h + 1) * 128] = block.reshape(1024, 128)
+        for ri in range(2):
+            for part in range(2):
+                start = ri * 512 + part * 256
+                got = dot(fwd[start : start + 256, :], rhs[...]).astype(BF16).reshape(16, 16, 256)
+                for h in range(2):
+                    spec[part * 16 : (part + 1) * 16, 2 * j + h, :, ri * 128 : (ri + 1) * 128] = got[
+                        :, :, h * 128 : (h + 1) * 128
+                    ]
+
+    @pl.loop(0, 32, unroll=4)
+    def _(slot):
+        val = spec[slot].reshape(128, 256)
+        mixed[slot] = mix_apply(val, mix_matrix(mix, slot), adjoint).reshape(8, 16, 256)
+        if accumulate is not None:
+            accumulate(slot, val)
+
+    @pl.loop(0, 4)
+    def _(j):
+        for h in range(2):
+            for ri in range(2):
+                rhs[ri * 512 : (ri + 1) * 512, h * 128 : (h + 1) * 128] = mixed[
+                    :, 2 * j + h, :, ri * 128 : (ri + 1) * 128
+                ].reshape(512, 128)
+        for part in range(4):
+            got = dot(inv[part * 256 : (part + 1) * 256, :], rhs[...]).astype(BF16)
+            for h in range(2):
+                piece = got[:, h * 128 : (h + 1) * 128].reshape(2, 8, 16, 128)
+                if axis == "x":
+                    out[part * 2 : (part + 1) * 2, j, h] = piece
+                else:
+                    out[2 * j + h, part] = piece
+
+
+def planes_adjoint_kernel(values, fx, ix, fy, iy, mix_x, mix_y, out, spec_x, spec_y, between, mixed, rhs):
+    line_pass("x", True, values, fx, ix, mix_x, between, spec_x, mixed, rhs)
+    line_pass("y", True, between, fy, iy, mix_y, out, spec_y, mixed, rhs)
+
+
+def planes_kernel(
+    values, fx, ix, fy, iy, mix_x, mix_y, cot_x, cot_y, table, out, terms, between, spec, mixed, rhs, sums
+):
+    lane = lax.broadcasted_iota(jnp.int32, (64, 128), 1)
+
+    def add_y(slot, val):
+        blocks = gradient_blocks(cot_y[slot].reshape(128, 256), val, slot)
+        for ri in range(2):
+            at = pl.ds(pl.multiple_of((ri * 32 + slot) * 64, 64), 64)
+            sums[at, :] = blocks[ri][64:] + pltpu.roll(blocks[ri][:64], 64, 1)
+
+    def add_x(slot, val):
+        blocks = gradient_blocks(cot_x[slot].reshape(128, 256), val, slot)
+        for ri in range(2):
+            at = pl.ds(pl.multiple_of((ri * 32 + slot) * 64, 64), 64)
+            got = blocks[ri][:64] + pltpu.roll(blocks[ri][64:], 64, 1)
+            sums[at, :] = jnp.where(lane < 64, got, sums[at, :])
+
+    line_pass("y", False, values, fy, iy, mix_y, between, spec, mixed, rhs, add_y)
+    line_pass("x", False, between, fx, ix, mix_x, out, spec, mixed, rhs, add_x)
+    to_lags(table, sums, terms)
+
+
+SPEC = (32, 8, 16, 256)
+
+
+def planes_adjoint(values, fx, ix, fy, iy, mix_x, mix_y):
+    spec = jax.ShapeDtypeStruct(SPEC, BF16)
+    return pl.pallas_call(
+        planes_adjoint_kernel,
+        out_shape=(jax.ShapeDtypeStruct(values.shape, BF16), spec, spec),
+        in_specs=whole(7),
+        out_specs=tuple(whole(3)),
+        scratch_shapes=[
+            pltpu.VMEM(values.shape, BF16),
+            pltpu.VMEM(SPEC, BF16),
+            pltpu.VMEM((1024, 256), BF16),
+        ],
+        compiler_params=params(44),
+        cost_estimate=pl.CostEstimate(flops=10 << 30, bytes_accessed=24 << 20, transcendentals=0),
+        name="planes_adjoint",
+    )(values, fx, ix, fy, iy, mix_x, mix_y)
+
+
+def planes(values, fx, ix, fy, iy, mix_x, mix_y, cot_x, cot_y, table):
+    return pl.pallas_call(
+        planes_kernel,
+        out_shape=(
+            jax.ShapeDtypeStruct(values.shape, BF16),
+            jax.ShapeDtypeStruct((4096, 128), F32),
+        ),
+        in_specs=whole(10),
+        out_specs=tuple(whole(2)),
+        scratch_shapes=[
+            pltpu.VMEM(values.shape, BF16),
+            pltpu.VMEM(SPEC, BF16),
+            pltpu.VMEM(SPEC, BF16),
+            pltpu.VMEM((1024, 256), BF16),
+            pltpu.VMEM((4096, 128), F32),
+        ],
+        compiler_params=params(44),
+        cost_estimate=pl.CostEstimate(flops=12 << 30, bytes_accessed=28 << 20, transcendentals=0),
+        name="planes",
+    )(values, fx, ix, fy, iy, mix_x, mix_y, cot_x, cot_y, table)
+
+
+def depth_pass(adjoint, values, fwd, inv, mix, out, spec, mixed, rhs, accumulate=None):
+    @pl.loop(0, 8)
+    def _(j):
+        for h in range(2):
+            lanes = slice(h * 128, (h + 1) * 128)
+            if adjoint:
+                rhs[:, lanes] = values[:, 2 * j + h].reshape(512, 128)
+            else:
+                for zp in range(32):
+                    rhs[zp * 16 : (zp + 1) * 16, lanes] = values[2 * j + h, :, zp * 128 : (zp + 1) * 128]
+        for ri in range(2):
+            got = dot(fwd[ri * 256 : (ri + 1) * 256, :], rhs[...]).astype(BF16).reshape(16, 16, 256)
+            for h in range(2):
+                spec[:, 2 * j + h, :, ri * 128 : (ri + 1) * 128] = got[:, :, h * 128 : (h + 1) * 128]
+
+    @pl.loop(0, 16, unroll=4)
+    def _(slot):
+        val = spec[slot].reshape(256, 256)
+        mixed[slot] = mix_apply(val, mix_matrix(mix, slot), adjoint).reshape(16, 16, 256)
+        if accumulate is not None:
+            accumulate(slot, val)
+
+    @pl.loop(0, 8)
+    def _(j):
+        for h in range(2):
+            for ri in range(2):
+                rhs[ri * 256 : (ri + 1) * 256, h * 128 : (h + 1) * 128] = mixed[
+                    :, 2 * j + h, :, ri * 128 : (ri + 1) * 128
+                ].reshape(256, 128)
+        for part in range(2):
+            got = dot(inv[part * 256 : (part + 1) * 256, :], rhs[...]).astype(BF16)
+            for h in range(2):
+                lanes = slice(h * 128, (h + 1) * 128)
+                if adjoint:
+                    for zp in range(16):
+                        place = (part * 16 + zp) * 128
+                        out[2 * j + h, :, place : place + 128] = got[zp * 16 : (zp + 1) * 16, lanes]
+                else:
+                    out[part * 16 : (part + 1) * 16, 2 * j + h] = got[:, lanes].reshape(16, 16, 128)
+
+
+DEPTH_SPEC = (16, 16, 16, 256)
+
+
+def depth_kernel(values, fwd, inv, mix, out, spec, mixed, rhs):
+    depth_pass(False, values, fwd, inv, mix, out, spec, mixed, rhs)
+
+
+def depth_adjoint_kernel(values, fwd, inv, mix, other, table, out, terms, spec, mixed, rhs, sums):
+    lane = lax.broadcasted_iota(jnp.int32, (64, 128), 1)
+
+    def add_z(slot, val):
+        blocks = gradient_blocks(val, other[slot].reshape(256, 256), slot)
+        for ri in range(2):
+            top, bottom = blocks[ri][:64], pltpu.roll(blocks[ri][64:], 64, 1)
+            at = pl.multiple_of((ri * 16 + slot) * 64, 64)
+            sums[pl.ds(at, 64), :] = jnp.where(lane < 64, top, 0.0) + bottom
+            sums[pl.ds(at + 2048, 64), :] = jnp.where(lane < 64, 0.0, top)
+
+    depth_pass(True, values, fwd, inv, mix, out, spec, mixed, rhs, add_z)
+    to_lags(table, sums, terms)
+
+
+def depth(values, fwd, inv, mix):
+    return pl.pallas_call(
+        depth_kernel,
+        out_shape=(
+            jax.ShapeDtypeStruct((32, 16, 16, 128), BF16),
+            jax.ShapeDtypeStruct(DEPTH_SPEC, BF16),
+        ),
+        in_specs=whole(4),
+        out_specs=tuple(whole(2)),
+        scratch_shapes=[pltpu.VMEM(DEPTH_SPEC, BF16), pltpu.VMEM((512, 256), BF16)],
+        compiler_params=params(24),
+        cost_estimate=pl.CostEstimate(flops=4 << 30, bytes_accessed=10 << 20, transcendentals=0),
+        name="depth",
+    )(values, fwd, inv, mix)
+
+
+def depth_adjoint(values, fwd, inv, mix, other, table):
+    return pl.pallas_call(
+        depth_adjoint_kernel,
+        out_shape=(
+            jax.ShapeDtypeStruct((16, 16, 4096), BF16),
+            jax.ShapeDtypeStruct((2048, 128), F32),
+        ),
+        in_specs=whole(6),
+        out_specs=tuple(whole(2)),
+        scratch_shapes=[
+            pltpu.VMEM(DEPTH_SPEC, BF16),
+            pltpu.VMEM(DEPTH_SPEC, BF16),
+            pltpu.VMEM((512, 256), BF16),
+            pltpu.VMEM((4096, 128), F32),
+        ],
+        compiler_params=params(32),
+        cost_estimate=pl.CostEstimate(flops=6 << 30, bytes_accessed=12 << 20, transcendentals=0),
+        name="depth_adjoint",
+    )(values, fwd, inv, mix, other, table)
 
 
 def dft_tables(row_ids, col_ids, length):
     product = row_ids[:, None] * col_ids[None, :] % length
     angle = product.astype(jnp.float32) * (2.0 * math.pi / length)
     return (jnp.cos(angle), jnp.sin(angle))
+
+
+def log_terms(taps, row_ids, col_ids, length):
+    highest = lax.Precision.HIGHEST
+    diag_w = jnp.diagonal(taps.astype(jnp.float32), axis1=2, axis2=3)
+    cos_full, sin_full = dft_tables(row_ids, row_ids, length)
+    real_z = jnp.einsum("kt,atc->akc", cos_full, diag_w, precision=highest)
+    imag_z = -jnp.einsum("kt,atc->akc", sin_full, diag_w, precision=highest)
+    modulus = real_z * real_z + imag_z * imag_z
+    cos_cols, sin_cols = dft_tables(row_ids, col_ids, length)
+    summed = jnp.einsum("kt,akc->atc", cos_cols, real_z / modulus, precision=highest) - jnp.einsum(
+        "kt,akc->atc", sin_cols, imag_z / modulus, precision=highest
+    )
+    return summed / math.sqrt(length)
+
+
+def own_log_terms(taps, count_px):
+    all_ids = jnp.arange(N, dtype=jnp.int32)
+    slab_t = N // count_px
+    t_ids = lax.axis_index("px") * slab_t + jnp.arange(slab_t, dtype=jnp.int32)
+    return log_terms(taps, all_ids, t_ids, N)
+
+
+def finish_taps(summed, log_part, count_py):
+    slab_o = C // count_py
+    o_ids = lax.axis_index("py") * slab_o + jnp.arange(slab_o, dtype=jnp.int32)
+    channel_ids = jnp.arange(C, dtype=jnp.int32)
+    diagonal_sel = (channel_ids[None, :] == o_ids[:, None]).astype(jnp.float32)
+    keep_mask = (channel_ids[None, :] <= o_ids[:, None]).astype(jnp.float32)
+    return keep_mask * (summed - log_part[:, :, None, :] * diagonal_sel)
+
+
+def halve(values, dim, axis, bit):
+    count = lax.axis_size(axis)
+    mine = (lax.axis_index(axis) >> bit) & 1
+    keep = lax.dynamic_index_in_dim(values, mine, dim, keepdims=False)
+    send = lax.dynamic_index_in_dim(values, 1 - mine, dim, keepdims=False).astype(BF16)
+    got = lax.ppermute(send, axis, [(i, i ^ (1 << bit)) for i in range(count)])
+    return keep + got.astype(F32)
+
+
+def plane_device(field, cotangent, taps):
+    axes = ("px", "py")
+    count_px = lax.axis_size("px")
+    count_py = lax.axis_size("py")
+    shape = field.shape
+    count = count_px * count_py
+    column_shape = (count, 16, 16, 128)
+    plane_shape = (count_px, count_py, 2, 8, 16, 128)
+
+    def exchange(values):
+        return lax.all_to_all(values, axes, 0, 0, tiled=True)
+
+    cot_pairs = cotangent.reshape(16, 16, count, 128).transpose(2, 0, 1, 3)
+    cot_planes = exchange(cot_pairs).reshape(plane_shape)
+
+    small = real_dft(N) + real_dft(N // 2)
+    fx, ix, fy, iy, fz, iz = tables(*[jnp.asarray(v, BF16) for v in small])
+    mix_x, mix_y, mix_z = mixing(taps, jnp.asarray(line_table(), BF16), jnp.asarray(pair_table(), BF16))
+    direct, paired = [jnp.asarray(v, F32) for v in tap_tables()]
+
+    first, field_spec = depth(field.reshape(16, 16, 4096), fz, iz, mix_z)
+    first_planes = exchange(first).reshape(plane_shape)
+
+    fx_then, log_part = lax.optimization_barrier((fx, own_log_terms(taps, count_px)))
+    back_one, cot_spec, back_spec = planes_adjoint(cot_planes, fx_then, ix, fy, iy, mix_x, mix_y)
+    back_columns = exchange(back_one.reshape(column_shape))
+
+    out, terms_xy = planes(first_planes, fx, ix, fy, iy, mix_x, mix_y, cot_spec, back_spec, direct)
+    out_columns = exchange(out.reshape(column_shape))
+
+    grad_field, terms_z = depth_adjoint(back_columns, fz, iz, mix_z, field_spec, paired)
+    mapped = out_columns.transpose(1, 2, 0, 3).reshape(shape)
+
+    terms = jnp.concatenate([terms_xy.reshape(8, 8, N, 128), terms_z.reshape(8, 4, N, 128)], 1)
+    terms = terms.reshape(2, 2, 2, 12, 2, 2, 16, 128)
+    for dim, axis, bit in ((5, "py", 0), (4, "py", 1), (2, "px", 0), (1, "px", 1), (0, "px", 2)):
+        terms = halve(terms, dim, axis, bit)
+    along_z = terms[8:].reshape(4, 16, 2, C).transpose(0, 2, 1, 3).reshape(8, 16, C)
+    summed = jnp.stack([terms[:8, :, :C], terms[:8, :, C:], along_z], 0)
+    grad_taps = finish_taps(summed, log_part, count_py)
+    return (mapped, grad_field.reshape(shape), grad_taps)
 
 
 def along(values, table, position):
@@ -97,21 +633,7 @@
     )
 
 
-def log_terms(taps, row_ids, col_ids, length):
-    highest = lax.Precision.HIGHEST
-    diag_w = jnp.diagonal(taps.astype(jnp.float32), axis1=2, axis2=3)
-    cos_full, sin_full = dft_tables(row_ids, row_ids, length)
-    real_z = jnp.einsum("kt,atc->akc", cos_full, diag_w, precision=highest)
-    imag_z = -jnp.einsum("kt,atc->akc", sin_full, diag_w, precision=highest)
-    modulus = real_z * real_z + imag_z * imag_z
-    cos_cols, sin_cols = dft_tables(row_ids, col_ids, length)
-    summed = jnp.einsum("kt,akc->atc", cos_cols, real_z / modulus, precision=highest) - jnp.einsum(
-        "kt,akc->atc", sin_cols, imag_z / modulus, precision=highest
-    )
-    return summed / math.sqrt(length)
-
-
-def per_device(field, cotangent, taps):
+def line_device(field, cotangent, taps):
     batch_rows = field.shape[0]
     local_x = field.shape[1]
     local_y = field.shape[2]
@@ -180,10 +702,6 @@
     mapped = returned[:batch_rows]
     grad_field = returned[batch_rows:]
     data_scale = 1.0 / (float(N) ** 4 * math.sqrt(N))
-    slab_t = N // count_px
-    slab_o = C // count_py
-    t_ids = lax.axis_index("px") * slab_t + jnp.arange(slab_t, dtype=jnp.int32)
-    o_ids = lax.axis_index("py") * slab_o + jnp.arange(slab_o, dtype=jnp.int32)
     terms = (
         jnp.stack(
             [
@@ -201,19 +719,18 @@
     summed = lax.psum_scatter(
         summed.astype(jnp.bfloat16), "py", scatter_dimension=2, tiled=True
     ).astype(jnp.float32)
-    log_part = log_terms(taps, all_ids, t_ids, N)
-    channel_ids = jnp.arange(C, dtype=jnp.int32)
-    diagonal_sel = (channel_ids[None, :] == o_ids[:, None]).astype(jnp.float32)
-    keep_mask = (channel_ids[None, :] <= o_ids[:, None]).astype(jnp.float32)
-    grad_taps = keep_mask * (summed - log_part[:, :, None, :] * diagonal_sel)
+    grad_taps = finish_taps(summed, own_log_terms(taps, count_px), count_py)
     return (mapped, grad_field, grad_taps)
 
 
 def solution(mesh):
+    count_px, count_py = mesh.shape["px"], mesh.shape["py"]
+    fits = N * C == 128 * count_px * count_py and N == 8 * count_px and N == 16 * count_py
+    spec = P(None, "px", "py", None)
     return jax.shard_map(
-        per_device,
+        plane_device if fits else line_device,
         mesh=mesh,
-        in_specs=(P(None, "px", "py", None), P(None, "px", "py", None), P()),
-        out_specs=(P(None, "px", "py", None), P(None, "px", "py", None), P(None, "px", "py", None)),
+        in_specs=(spec, spec, P()),
+        out_specs=(spec, spec, spec),
         check_vma=False,
     )

time: 982 us -> 238 us (0.24)
  waiting for transfers between devices: 422 us -> 56 us
  matrix products: 206 us -> 1.44 us
  blocking collectives: 101 us -> 0 us
  Pallas kernels: 0 us -> 97.1 us
  local copies, waits for them, and re-layouts: 132 us -> 43.9 us
  other arithmetic: 79.9 us -> 4.56 us
  starting transfers between devices: 18.4 us -> 33 us
  between operations: 14.9 us -> 0.99 us
    all_to_all x3 -> x4, waiting for transfers between devices: 338 us -> 32.6 us  [exchange(): return lax.all_to_all(values, axes, 0, 0, tiled=True)]
    dot_general x33 -> x0, matrix products: 205 us -> none  [the longest x12 144 us: along(): jnp.einsum(letters + ',k' + letters[position] + '->' + target, values, ta...]
    all_to_all x1 -> x0, blocking collectives: 101 us -> none  [per_device(): lax.all_to_all(spectral, 'py', split_axis=3, concat_axis=2, tiled=True)]
    pallas_call x0 -> x6, Pallas kernels: none -> 97.1 us  [the longest x1 30.7 us: planes(): pl.pallas_call(planes_kernel, out_shape=(jax.ShapeDtypeStruct(values.shap...]
    reduce_scatter x2 -> x0, waiting for transfers between devices: 84.6 us -> none  [the longest x1 64.1 us: per_device(): lax.psum_scatter(terms.astype(jnp.bfloat16), 'px', scatter_dimension=1, t...]
    slice x4 -> x0, other arithmetic: 49.4 us -> none  [section(): turned = jnp.concatenate([crossed[..., half:], -crossed[..., :half]], -1)]
    convert_element_type x4, local copies, waits for them, and re-layouts: 41.6 us -> 0.13 us  [halve(): lax.dynamic_index_in_dim(values, 1 - mine, dim, keepdims=False).astype(BF16)]
    slice x4 -> x1, local copies, waits for them, and re-layouts: 25 us -> 0.01 us  [plane_device(): terms[8:].reshape(4, 16, 2, C).transpose(0, 2, 1, 3).reshape(8, 16, C)]
  transfers between devices with their start and end apart: 5 -> 9, of which waited for: 4 -> 7; matrix products, arithmetic and copies ran while one was open for 7% -> 8% of each run, Pallas kernels for 0% -> 41%
where the time goes in v1:
time: 238 us; the launch traced here: 237 us
  Pallas kernels  97.1 us (41%)
  waiting for transfers between devices  56 us (24%)
  local copies, waits for them, and re-layouts  43.9 us (18%)
  starting transfers between devices  33 us (14%)
  other arithmetic  4.56 us (2%)
    unnamed x62, local copies, waits for them, and re-layouts  33.2 us
    all_to_all x4, waiting for transfers between devices, exchange(): return lax.all_to_all(values, axes, 0, 0, tiled=True)  32.6 us
    pallas_call x1, Pallas kernels, planes(): pl.pallas_call(planes_kernel, out_shape=(jax.ShapeDtypeStruct(values.shap...  30.7 us
    ppermute x5, waiting for transfers between devices, halve(): got = lax.ppermute(send, axis, [(i, i ^ 1 << bit) for i in range(count)])  23.4 us
    pallas_call x1, Pallas kernels, planes_adjoint(): pl.pallas_call(planes_adjoint_kernel, out_shape=(jax.ShapeDtypeStruct(val...  23.4 us
    all_to_all x4, starting transfers between devices, exchange(): return lax.all_to_all(values, axes, 0, 0, tiled=True)  20.2 us
    pallas_call x1, Pallas kernels, mixing(): pl.pallas_call(mixing_kernel, out_shape=(line, line, pair), in_specs=whol...  15 us
    pallas_call x1, Pallas kernels, depth_adjoint(): pl.pallas_call(depth_adjoint_kernel, out_shape=(jax.ShapeDtypeStruct((16,...  13 us
  transfers between devices with their start and end apart: 9, of which 7 were waited for; matrix products, arithmetic and copies ran while one was open for 8% of the time, Pallas kernels for 41%

profile of v1, /device:TPU:0, one launch (start us, length us, event | category | flops | bytes accessed | tf_op | source)
XLA Modules:
  0.0 237.0 jit_solution(4699650661262552531)
XLA Ops:
  0.6 2.1 copy.36
  2.7 2.1 copy.48
  4.8 7.5 %all-to-all-start.1 = ((bf16[32,16,16,128]{3,2,1,0:T(8,128)(2,1)}), bf16[32,16,16,128]{3,2,1,0:T(8,128)(2,1)}, u32[]{:S(2)}, u32[]{:S(2)}) async-start(bf16[32,16,16,128]{3,2,1,0:T(8,128)(2,1)} %bitcast.84), calls=%async_computation.1 | async-start | bytes 4194304 | tf_op jit(solution)/shard_map/all_to_all | solution.py:521
  12.4 15.0 %mixing.1 = (bf16[2,2,32,128,128]{4,3,2,1,0:T(8,128)(2,1)S(1)}, bf16[2,2,32,128,128]{4,3,2,1,0:T(8,128)(2,1)S(1)}, bf16[2,2,16,128,128]{4,3,2,1,0:T(8,128)(2,1)S(1)}) custom-call(bf16[3,64,64,64]{3,2,1,0:T(8,128)(2,1)S(1)} %copy-done, bf16[72,64]{1,0:T(8,128)(2,1)S(1)} %copy-done.6, bf16[128,128]{1,0:T(8,128)(2,1)S(1)} %copy-done.5), custom_call_target="tpu_custom_call" | custom-call | flops 2147483648 | bytes 12582912 | tf_op jit(solution)/shard_map/mixing/pallas_call | solution.py:208
  27.4 1.9 copy-done.12
  29.3 2.0 copy-done.13
  31.4 8.7 %tables.1 = (bf16[1024,1024]{1,0:T(8,128)(2,1)S(1)}, bf16[1024,1024]{1,0:T(8,128)(2,1)S(1)}, bf16[1024,1024]{1,0:T(8,128)(2,1)S(1)}, bf16[1024,1024]{1,0:T(8,128...) custom-call(bf16[64,64]{1,0:T(8,128)(2,1)S(1)} %copy-done.9, bf16[64,64]{1,0:T(8,128)(2,1)S(1)} %copy-done.8, ...), custom_call_target="tpu_custom_call" | custom-call | flops 2147483648 | bytes 12582912 | tf_op jit(solution)/shard_map/tables/pallas_call | solution.py:147
  40.1 1.3 copy-done.16
  41.4 1.3 copy-done.18
  42.8 1.3 copy-done.19
  44.1 1.3 copy-done.20
  45.5 6.4 %depth.1 = (bf16[32,16,16,128]{3,2,1,0:T(8,128)(2,1)S(1)}, bf16[16,16,16,256]{3,2,1,0:T(8,128)(2,1)S(1)}) custom-call(bf16[16,16,4096]{2,1,0:T(8,128)(2,1)S(1)} %bitcast.83, bf16[512,512]{1,0:T(8,128)(2,1)S(1)} %get-tuple-element.23.fwd, bf16[512,512]{1,0:T(8,128)(2,1)S(1)} %get-tuple-element.24.inv, bf16[2,2,16,128,128]{4,3,2,1,0:T(8,128)(2,1)S(1)} %get-tuple-element.25.mix), custom_call_target="tpu_custom_call" | custom-call | flops 4294967296 | bytes 10485760 | tf_op jit(solution)/shard_map/depth/pallas_call | solution.py:430
  51.9 1.3 copy-done.2
  53.2 1.3 copy-done.21
  55.3 0.8 copy-done.25
  56.1 4.9 %all-to-all-done.1 = bf16[32,16,16,128]{3,2,1,0:T(8,128)(2,1)} async-done(((bf16[32,16,16,128]{3,2,1,0:T(8,128)(2,1)}), bf16[32,16,16,128]{3,2,1,0:T(8,128)(2,1)}, u32[]{:S(2)}, u32[]{:S(2)}) %all-to-all-start.1) | async-done | bytes 2097184 | tf_op jit(solution)/shard_map/all_to_all | solution.py:521
  61.0 4.2 %all-to-all-start = ((bf16[32,16,16,128]{3,2,1,0:T(8,128)(2,1)}), bf16[32,16,16,128]{3,2,1,0:T(8,128)(2,1)}, u32[]{:S(2)}, u32[]{:S(2)}) async-start(bf16[32,16,16,128]{3,2,1,0:T(8,128)(2,1)} %copy-done.2), calls=%async_computation | async-start | bytes 4194304 | tf_op jit(solution)/shard_map/all_to_all | solution.py:521
  65.2 5.4 %copy.22 = bf16[3,64,64,64]{1,0,3,2:T(4,128)(2,1)} copy(bf16[3,64,64,64]{3,2,1,0:T(8,128)(2,1)S(1)} %copy-done) | data formatting | bytes 3145728 | tf_op args[2]
  70.7 2.9 %gather_fusion = bf16[64,3,64]{2,1,0:T(4,128)(2,1)S(1)} fusion(bf16[3,64,64,64]{1,0,3,2:T(4,128)(2,1)} %copy.22, s32[64]{0:T(128)S(1)} %or_bitcast_fusion), kind=kCustom, calls=%fused_computation | custom fusion | bytes 49664 | tf_op jit(solution)/shard_map/jit(diagonal)/gather | solution.py:474
  75.1 23.4 %planes_adjoint.1 = (bf16[8,4,2,8,16,128]{5,4,3,2,1,0:T(8,128)(2,1)}, bf16[32,8,16,256]{3,2,1,0:T(8,128)(2,1)S(1)}, bf16[32,8,16,256]{3,2,1,0:T(8,128)(2,1)S(1)}) custom-call(bf16[8,4,2,8,16,128]{5,4,3,2,1,0:T(8,128)(2,1)} %bitcast.3.values, bf16[1024,1024]{1,0:T(8,128)(2,1)} %copy-done.16, bf16[1024,1024]{1,0:T(8,128)(2,1)} %copy-done.18, ...), custom_call_target="tpu_custom_call" | custom-call | flops 10737418240 | bytes 25165824 | tf_op jit(solution)/shard_map/planes_adjoint/pallas_call | solution.py:328
  98.5 1.4 copy-done.27
  99.9 1.4 copy-done.28
  101.3 12.6 %all-to-all-done = bf16[32,16,16,128]{3,2,1,0:T(8,128)(2,1)} async-done(((bf16[32,16,16,128]{3,2,1,0:T(8,128)(2,1)}), bf16[32,16,16,128]{3,2,1,0:T(8,128)(2,1)}, u32[]{:S(2)}, u32[]{:S(2)}) %all-to-all-start) | async-done | bytes 2097184 | tf_op jit(solution)/shard_map/all_to_all | solution.py:521
  114.0 4.4 %all-to-all-start.3 = ((bf16[32,16,16,128]{3,2,1,0:T(8,128)(2,1)}), bf16[32,16,16,128]{3,2,1,0:T(8,128)(2,1)}, u32[]{:S(2)}, u32[]{:S(2)}) async-start(bf16[32,16,16,128]{3,2,1,0:T(8,128)(2,1)} %bitcast.16), calls=%async_computation.3 | async-start | bytes 4194304 | tf_op jit(solution)/shard_map/all_to_all | solution.py:521
  118.4 1.6 copy-done.17
  120.0 30.7 %planes.1 = (bf16[8,4,2,8,16,128]{5,4,3,2,1,0:T(8,128)(2,1)S(1)}, f32[4096,128]{1,0:T(8,128)S(1)}) custom-call(bf16[8,4,2,8,16,128]{5,4,3,2,1,0:T(8,128)(2,1)} %bitcast.1.values, bf16[1024,1024]{1,0:T(8,128)(2,1)S(1)} %copy-done.17, bf16[1024,1024]{1,0:T(8,128)(2,1)} %copy-done.18, bf16[1024,1024]{1,0:T(8,128)(2,1)} %copy-done.19, ...), custom_call_target="tpu_custom_call" | custom-call | flops 12884901888 | bytes 29360128 | tf_op jit(solution)/shard_map/planes/pallas_call | solution.py:345
  150.7 1.3 copy-done.1
  152.0 15.0 %all-to-all-done.3.values = bf16[32,16,16,128]{3,2,1,0:T(8,128)(2,1)} async-done(((bf16[32,16,16,128]{3,2,1,0:T(8,128)(2,1)}), bf16[32,16,16,128]{3,2,1,0:T(8,128)(2,1)}, u32[]{:S(2)}, u32[]{:S(2)}) %all-to-all-start.3) | async-done | bytes 2097184 | tf_op jit(solution)/shard_map/all_to_all | solution.py:521
  167.0 4.1 %all-to-all-start.2 = ((bf16[32,16,16,128]{3,2,1,0:T(8,128)(2,1)}), bf16[32,16,16,128]{3,2,1,0:T(8,128)(2,1)}, u32[]{:S(2)}, u32[]{:S(2)}) async-start(bf16[32,16,16,128]{3,2,1,0:T(8,128)(2,1)} %bitcast.82), calls=%async_computation.2 | async-start | bytes 4194304 | tf_op jit(solution)/shard_map/all_to_all | solution.py:521
  171.2 1.6 copy-done.15
  172.7 1.6 copy-done.22
  174.3 1.0 copy-done.24
  175.4 1.0 copy-done.26
  176.4 13.0 %depth_adjoint.1 = (bf16[16,16,4096]{2,1,0:T(8,128)(2,1)}, f32[2048,128]{1,0:T(8,128)S(1)}) custom-call(bf16[32,16,16,128]{3,2,1,0:T(8,128)(2,1)} %all-to-all-done.3.values, bf16[512,512]{1,0:T(8,128)(2,1)S(1)} %copy-done.24, bf16[512,512]{1,0:T(8,128)(2,1)S(1)} %copy-done.26, bf16[2,2,16,128,128]{4,3,2,1,0:T(8,128)(2,1)S(1)} %copy-done.15, ...), custom_call_target="tpu_custom_call" | custom-call | flops 6442450944 | bytes 12582912 | tf_op jit(solution)/shard_map/depth_adjoint/pallas_call | solution.py:446
  189.4 1.1 fusion.5
  190.7 2.5 %collective-permute-done = bf16[2,2,2,12,2,16,128]{6,5,3,0,1,2,4:T(8,128)(2,1)} collective-permute-done((bf16[2,2,2,12,2,16,128]{6,5,3,0,1,2,4:T(8,128)(2,1)}, bf16[2,2,2,12,2,16,128]{6,5,3,0,1,2,4:T(8,128)(2,1)}, u32[]{:S(2)}, u32[]{:S(2)}) %collective-permute-start) | collective-permute-done | bytes 786464 | tf_op jit(solution)/shard_map/ppermute | solution.py:507
  193.1 1.4 fusion.2
  194.5 1.2 copy-done.29
  195.7 1.7 collective-permute-start.1
  197.5 11.0 %collective-permute-done.1 = bf16[2,2,2,12,16,128]{5,4,3,0,1,2:T(8,128)(2,1)S(1)} collective-permute-done((bf16[2,2,2,12,16,128]{5,4,3,0,1,2:T(8,128)(2,1)S(1)}, bf16[2,2,2,12,16,128]{5,4,3,0,1,2:T(8,128)(2,1)S(1)}, u32[]{:S(2)}, u32[]{:S(2)}) %collective-permute-start.1) | collective-permute-done | bytes 393248 | tf_op jit(solution)/shard_map/ppermute | solution.py:507
  208.4 1.2 bitcast_add_fusion
  209.7 1.0 collective-permute-start.2
  210.7 7.4 %collective-permute-done.2 = bf16[2,2,12,16,128]{4,3,2,0,1:T(8,128)(2,1)S(1)} collective-permute-done((bf16[2,2,12,16,128]{4,3,2,0,1:T(8,128)(2,1)S(1)}, bf16[2,2,12,16,128]{4,3,2,0,1:T(8,128)(2,1)S(1)}, u32[]{:S(2)}, u32[]{:S(2)}) %collective-permute-start.2) | collective-permute-done | bytes 196640 | tf_op jit(solution)/shard_map/ppermute | solution.py:507
  218.2 4.1 %collective-permute-start.3 = (bf16[2,12,16,128]{3,2,1,0:T(8,128)(2,1)S(1)}, bf16[2,12,16,128]{3,2,1,0:T(8,128)(2,1)S(1)}, u32[]{:S(2)}, u32[]{:S(2)}) collective-permute-start(bf16[2,12,16,128]{3,2,1,0:T(8,128)(2,1)S(1)} %fusion.9), channel_id=1, source_target_pairs={{0,8},{4,12},{8,0},{12,4},{16,24},{20,28},{24,16},{28,20},{1,9},{5... | collective-permute-start | bytes 294920 | tf_op jit(solution)/shard_map/ppermute | solution.py:507
  222.3 2.6 %collective-permute-done.3 = bf16[2,12,16,128]{3,2,1,0:T(8,128)(2,1)S(1)} collective-permute-done((bf16[2,12,16,128]{3,2,1,0:T(8,128)(2,1)S(1)}, bf16[2,12,16,128]{3,2,1,0:T(8,128)(2,1)S(1)}, u32[]{:S(2)}, u32[]{:S(2)}) %collective-permute-start.3) | collective-permute-done | bytes 98336 | tf_op jit(solution)/shard_map/ppermute | solution.py:507
  225.0 5.8 %collective-permute-start.4 = (bf16[12,16,128]{2,1,0:T(8,128)(2,1)S(1)}, bf16[12,16,128]{2,1,0:T(8,128)(2,1)S(1)}, u32[]{:S(2)}, u32[]{:S(2)}) collective-permute-start(bf16[12,16,128]{2,1,0:T(8,128)(2,1)S(1)} %fusion.14), channel_id=1, source_target_pairs={{0,16},{4,20},{8,24},{12,28},{16,0},{20,4},{24,8},{28,12},{1,17},{... | collective-permute-start | bytes 147464 | tf_op jit(solution)/shard_map/ppermute | solution.py:507
  230.8 2.9 %copy.27 = bf16[16,16,32,128]{3,2,1,0:T(8,128)(2,1)S(1)} copy(bf16[16,16,32,128]{3,1,0,2:T(8,128)(2,1)} %bitcast.15) | data formatting | bytes 4194304 | tf_op jit(solution)/shard_map/transpose | solution.py:542
  233.8 2.3 reshape.99
  (65 shorter events, 3.7 us)
Async XLA Ops:
  4.8 7.5 %copy-start = (bf16[3,64,64,64]{3,2,1,0:T(8,128)(2,1)S(1)}, bf16[3,64,64,64]{3,2,1,0:T(8,128)(2,1)}, u32[]{:S(2)}) copy-start(bf16[3,64,64,64]{3,2,1,0:T(8,128)(2,1)} %taps.1) | copy-start | bytes 4718596
  4.8 7.5 %copy-start.5 = (bf16[128,128]{1,0:T(8,128)(2,1)S(1)}, bf16[128,128]{1,0:T(8,128)(2,1)}, u32[]{:S(2)}) copy-start(bf16[128,128]{1,0:T(8,128)(2,1)} %constant.109.clone.e_pair) | copy-start | bytes 98308
  4.8 7.5 %copy-start.6 = (bf16[72,64]{1,0:T(8,128)(2,1)S(1)}, bf16[72,64]{1,0:T(8,128)(2,1)}, u32[]{:S(2)}) copy-start(bf16[72,64]{1,0:T(8,128)(2,1)} %constant.108.clone.e_line) | copy-start | bytes 27652
  4.8 56.2 %all-to-all-start.1 = ((bf16[32,16,16,128]{3,2,1,0:T(8,128)(2,1)}), bf16[32,16,16,128]{3,2,1,0:T(8,128)(2,1)}, u32[]{:S(2)}, u32[]{:S(2)}) async-start(bf16[32,16,16,128]{3,2,1,0:T(8,128)(2,1)} %bitcast.84), calls=%async_computation.1 | async-start | bytes 4194304 | tf_op jit(solution)/shard_map/all_to_all | solution.py:521
  12.3 19.0 %copy-start.8 = (bf16[64,64]{1,0:T(8,128)(2,1)S(1)}, bf16[64,64]{1,0:T(8,128)(2,1)}, u32[]{:S(2)}) copy-start(bf16[64,64]{1,0:T(8,128)(2,1)} %constant.105.clone.inv) | copy-start | bytes 24580
  12.3 19.0 %copy-start.9 = (bf16[64,64]{1,0:T(8,128)(2,1)S(1)}, bf16[64,64]{1,0:T(8,128)(2,1)}, u32[]{:S(2)}) copy-start(bf16[64,64]{1,0:T(8,128)(2,1)} %constant.104.clone.fwd) | copy-start | bytes 24580
  12.4 19.0 %copy-start.10 = (bf16[32,32]{1,0:T(8,128)(2,1)S(1)}, bf16[32,32]{1,0:T(8,128)(2,1)}, u32[]{:S(2)}) copy-start(bf16[32,32]{1,0:T(8,128)(2,1)} %constant.107.clone.inv_z) | copy-start | bytes 6148
  12.4 19.0 %copy-start.11 = (bf16[32,32]{1,0:T(8,128)(2,1)S(1)}, bf16[32,32]{1,0:T(8,128)(2,1)}, u32[]{:S(2)}) copy-start(bf16[32,32]{1,0:T(8,128)(2,1)} %constant.106.clone.fwd_z) | copy-start | bytes 6148
  27.4 2.0 copy-start.12
  29.3 2.0 copy-start.13
  31.4 14.1 %copy-start.14 = (bf16[2,2,16,128,128]{4,3,2,1,0:T(8,128)(2,1)}, bf16[2,2,16,128,128]{4,3,2,1,0:T(8,128)(2,1)S(1)}, u32[]{:S(2)}) copy-start(bf16[2,2,16,128,128]{4,3,2,1,0:T(8,128)(2,1)S(1)} %get-tuple-element.25.mix) | copy-start | bytes 6291460
  31.4 14.1 %copy-start.3 = (bf16[2,8,16,4096]{3,2,1,0:T(8,128)(2,1)S(1)}, bf16[2,8,16,4096]{3,2,1,0:T(8,128)(2,1)}, u32[]{:S(2)}) copy-start(bf16[2,8,16,4096]{3,2,1,0:T(8,128)(2,1)} %param.11) | copy-start | bytes 6291460
  40.1 1.3 copy-start.16
  41.4 1.3 copy-start.18
  42.8 1.3 copy-start.19
  44.1 1.4 copy-start.20
  51.8 1.3 copy-start.2
  53.2 1.3 copy-start.21
  54.5 0.8 copy-start.23
  55.3 0.8 copy-start.25
  61.0 52.9 %all-to-all-start = ((bf16[32,16,16,128]{3,2,1,0:T(8,128)(2,1)}), bf16[32,16,16,128]{3,2,1,0:T(8,128)(2,1)}, u32[]{:S(2)}, u32[]{:S(2)}) async-start(bf16[32,16,16,128]{3,2,1,0:T(8,128)(2,1)} %copy-done.2), calls=%async_computation | async-start | bytes 4194304 | tf_op jit(solution)/shard_map/all_to_all | solution.py:521
  98.5 1.4 copy-start.27
  99.9 1.4 copy-start.28
  114.0 4.4 %copy-start.4 = (f32[64,64]{1,0:T(8,128)S(1)}, f32[64,64]{1,0:T(8,128)}, u32[]{:S(2)}) copy-start(f32[64,64]{1,0:T(8,128)} %constant.110.clone.table) | copy-start | bytes 49156
  114.0 53.1 %all-to-all-start.3 = ((bf16[32,16,16,128]{3,2,1,0:T(8,128)(2,1)}), bf16[32,16,16,128]{3,2,1,0:T(8,128)(2,1)}, u32[]{:S(2)}, u32[]{:S(2)}) async-start(bf16[32,16,16,128]{3,2,1,0:T(8,128)(2,1)} %bitcast.16), calls=%async_computation.3 | async-start | bytes 4194304 | tf_op jit(solution)/shard_map/all_to_all | solution.py:521
  118.4 1.6 copy-start.17
  150.7 1.3 copy-start.1
  167.0 4.1 %copy-start.7 = (f32[32,64]{1,0:T(8,128)S(1)}, f32[32,64]{1,0:T(8,128)}, u32[]{:S(2)}) copy-start(f32[32,64]{1,0:T(8,128)} %constant.111.clone.table) | copy-start | bytes 24580
  167.0 63.8 %all-to-all-start.2 = ((bf16[32,16,16,128]{3,2,1,0:T(8,128)(2,1)}), bf16[32,16,16,128]{3,2,1,0:T(8,128)(2,1)}, u32[]{:S(2)}, u32[]{:S(2)}) async-start(bf16[32,16,16,128]{3,2,1,0:T(8,128)(2,1)} %bitcast.82), calls=%async_computation.2 | async-start | bytes 4194304 | tf_op jit(solution)/shard_map/all_to_all | solution.py:521
  171.1 1.6 copy-start.15
  172.7 1.6 copy-start.22
  174.3 1.0 copy-start.24
  175.4 1.0 copy-start.26
  190.5 2.6 %collective-permute-start = (bf16[2,2,2,12,2,16,128]{6,5,3,0,1,2,4:T(8,128)(2,1)}, bf16[2,2,2,12,2,16,128]{6,5,3,0,1,2,4:T(8,128)(2,1)}, u32[]{:S(2)}, u32[]{:S(2)}) collective-permute-start(bf16[2,2,2,12,2,16,128]{6,5,3,0,1,2,4:T(8,128)(2,1)} %fusion.5), channel_id=1, source_target_pairs={{0,1},{1,0},{2,3},{3,2},{4,5},{5,4},{6,7},{7,6},{8,9},{9,8},{10,11... | collective-permute-start | bytes 2359304 | tf_op jit(solution)/shard_map/ppermute | solution.py:507
  194.5 1.2 copy-start.29
  195.7 12.7 %collective-permute-start.1 = (bf16[2,2,2,12,16,128]{5,4,3,0,1,2:T(8,128)(2,1)S(1)}, bf16[2,2,2,12,16,128]{5,4,3,0,1,2:T(8,128)(2,1)S(1)}, u32[]{:S(2)}, u32[]{:S(2)}) collective-permute-start(bf16[2,2,2,12,16,128]{5,4,3,0,1,2:T(8,128)(2,1)S(1)} %fusion.6), channel_id=1, source_target_pairs={{0,2},{1,3},{2,0},{3,1},{4,6},{5,7},{6,4},{7,5},{8,10},{9,11},{10,... | collective-permute-start | bytes 1179656 | tf_op jit(solution)/shard_map/ppermute | solution.py:507
  209.7 8.4 %collective-permute-start.2 = (bf16[2,2,12,16,128]{4,3,2,0,1:T(8,128)(2,1)S(1)}, bf16[2,2,12,16,128]{4,3,2,0,1:T(8,128)(2,1)S(1)}, u32[]{:S(2)}, u32[]{:S(2)}) collective-permute-start(bf16[2,2,12,16,128]{4,3,2,0,1:T(8,128)(2,1)S(1)} %fusion.7), channel_id=1, source_target_pairs={{0,4},{4,0},{8,12},{12,8},{16,20},{20,16},{24,28},{28,24},{1,5},{5... | collective-permute-start | bytes 589832 | tf_op jit(solution)/shard_map/ppermute | solution.py:507
  218.2 6.7 %collective-permute-start.3 = (bf16[2,12,16,128]{3,2,1,0:T(8,128)(2,1)S(1)}, bf16[2,12,16,128]{3,2,1,0:T(8,128)(2,1)S(1)}, u32[]{:S(2)}, u32[]{:S(2)}) collective-permute-start(bf16[2,12,16,128]{3,2,1,0:T(8,128)(2,1)S(1)} %fusion.9), channel_id=1, source_target_pairs={{0,8},{4,12},{8,0},{12,4},{16,24},{20,28},{24,16},{28,20},{1,9},{5... | collective-permute-start | bytes 294920 | tf_op jit(solution)/shard_map/ppermute | solution.py:507
  225.0 11.1 %collective-permute-start.4 = (bf16[12,16,128]{2,1,0:T(8,128)(2,1)S(1)}, bf16[12,16,128]{2,1,0:T(8,128)(2,1)S(1)}, u32[]{:S(2)}, u32[]{:S(2)}) collective-permute-start(bf16[12,16,128]{2,1,0:T(8,128)(2,1)S(1)} %fusion.14), channel_id=1, source_target_pairs={{0,16},{4,20},{8,24},{12,28},{16,0},{20,4},{24,8},{28,12},{1,17},{... | collective-permute-start | bytes 147464 | tf_op jit(solution)/shard_map/ppermute | solution.py:507

commit v2 on v1

--- a/solution.py
+++ b/solution.py
@@ -363,7 +363,7 @@
     )(values, fx, ix, fy, iy, mix_x, mix_y, cot_x, cot_y, table)
 
 
-def depth_pass(adjoint, values, fwd, inv, mix, out, spec, mixed, rhs, accumulate=None):
+def depth_forward(adjoint, values, fwd, spec, rhs):
     @pl.loop(0, 8)
     def _(j):
         for h in range(2):
@@ -378,12 +378,12 @@
             for h in range(2):
                 spec[:, 2 * j + h, :, ri * 128 : (ri + 1) * 128] = got[:, :, h * 128 : (h + 1) * 128]
 
+
+def depth_backward(adjoint, spec, inv, mix, out, mixed, rhs):
     @pl.loop(0, 16, unroll=4)
     def _(slot):
         val = spec[slot].reshape(256, 256)
         mixed[slot] = mix_apply(val, mix_matrix(mix, slot), adjoint).reshape(16, 16, 256)
-        if accumulate is not None:
-            accumulate(slot, val)
 
     @pl.loop(0, 8)
     def _(j):
@@ -408,13 +408,18 @@
 
 
 def depth_kernel(values, fwd, inv, mix, out, spec, mixed, rhs):
-    depth_pass(False, values, fwd, inv, mix, out, spec, mixed, rhs)
-
-
-def depth_adjoint_kernel(values, fwd, inv, mix, other, table, out, terms, spec, mixed, rhs, sums):
+    depth_forward(False, values, fwd, spec, rhs)
+    depth_backward(False, spec, inv, mix, out, mixed, rhs)
+
+
+def depth_sums_kernel(values, fwd, other, table, spec, terms, rhs, sums):
     lane = lax.broadcasted_iota(jnp.int32, (64, 128), 1)
 
-    def add_z(slot, val):
+    depth_forward(True, values, fwd, spec, rhs)
+
+    @pl.loop(0, 16, unroll=4)
+    def _(slot):
+        val = spec[slot].reshape(256, 256)
         blocks = gradient_blocks(val, other[slot].reshape(256, 256), slot)
         for ri in range(2):
             top, bottom = blocks[ri][:64], pltpu.roll(blocks[ri][64:], 64, 1)
@@ -422,8 +427,11 @@
             sums[pl.ds(at, 64), :] = jnp.where(lane < 64, top, 0.0) + bottom
             sums[pl.ds(at + 2048, 64), :] = jnp.where(lane < 64, 0.0, top)
 
-    depth_pass(True, values, fwd, inv, mix, out, spec, mixed, rhs, add_z)
     to_lags(table, sums, terms)
+
+
+def depth_adjoint_kernel(spec, inv, mix, out, mixed, rhs):
+    depth_backward(True, spec, inv, mix, out, mixed, rhs)
 
 
 def depth(values, fwd, inv, mix):
@@ -442,25 +450,88 @@
     )(values, fwd, inv, mix)
 
 
-def depth_adjoint(values, fwd, inv, mix, other, table):
+def depth_sums(values, fwd, other, table):
+    return pl.pallas_call(
+        depth_sums_kernel,
+        out_shape=(
+            jax.ShapeDtypeStruct(DEPTH_SPEC, BF16),
+            jax.ShapeDtypeStruct((2048, 128), F32),
+        ),
+        in_specs=whole(4),
+        out_specs=tuple(whole(2)),
+        scratch_shapes=[pltpu.VMEM((512, 256), BF16), pltpu.VMEM((4096, 128), F32)],
+        compiler_params=params(58),
+        cost_estimate=pl.CostEstimate(flops=4 << 30, bytes_accessed=8 << 20, transcendentals=0),
+        name="depth_sums",
+    )(values, fwd, other, table)
+
+
+def depth_adjoint(spec, inv, mix):
     return pl.pallas_call(
         depth_adjoint_kernel,
-        out_shape=(
-            jax.ShapeDtypeStruct((16, 16, 4096), BF16),
-            jax.ShapeDtypeStruct((2048, 128), F32),
-        ),
-        in_specs=whole(6),
-        out_specs=tuple(whole(2)),
+        out_shape=jax.ShapeDtypeStruct((16, 16, 4096), BF16),
+        in_specs=whole(3),
+        out_specs=whole(1)[0],
+        scratch_shapes=[pltpu.VMEM(DEPTH_SPEC, BF16), pltpu.VMEM((512, 256), BF16)],
+        compiler_params=params(24),
+        cost_estimate=pl.CostEstimate(flops=2 << 30, bytes_accessed=6 << 20, transcendentals=0),
+        name="depth_adjoint",
+    )(spec, inv, mix)
+
+
+def to_pairs_kernel(src, dst, wide, narrow, came, went):
+    arrivals = [pltpu.make_async_copy(src.at[k], wide.at[k], came.at[k]) for k in range(4)]
+    departures = [pltpu.make_async_copy(narrow.at[k], dst.at[:, k], went.at[k]) for k in range(4)]
+    for copy in arrivals:
+        copy.start()
+    for k in range(4):
+        arrivals[k].wait()
+        for zp in range(32):
+            narrow[k, zp] = wide[k, :, :, zp * 128 : (zp + 1) * 128]
+        departures[k].start()
+    for copy in departures:
+        copy.wait()
+
+
+def to_pairs(columns):
+    return pl.pallas_call(
+        to_pairs_kernel,
+        out_shape=jax.ShapeDtypeStruct((32, 4, 4, 16, 128), BF16),
+        in_specs=[pl.BlockSpec(memory_space=pltpu.HBM)],
+        out_specs=pl.BlockSpec(memory_space=pltpu.HBM),
         scratch_shapes=[
-            pltpu.VMEM(DEPTH_SPEC, BF16),
-            pltpu.VMEM(DEPTH_SPEC, BF16),
-            pltpu.VMEM((512, 256), BF16),
-            pltpu.VMEM((4096, 128), F32),
+            pltpu.VMEM((4, 4, 16, 4096), BF16),
+            pltpu.VMEM((4, 32, 4, 16, 128), BF16),
+            pltpu.SemaphoreType.DMA((4,)),
+            pltpu.SemaphoreType.DMA((4,)),
         ],
-        compiler_params=params(32),
-        cost_estimate=pl.CostEstimate(flops=6 << 30, bytes_accessed=12 << 20, transcendentals=0),
-        name="depth_adjoint",
-    )(values, fwd, inv, mix, other, table)
+        compiler_params=params(60),
+        cost_estimate=pl.CostEstimate(flops=0, bytes_accessed=4 << 20, transcendentals=0),
+        name="to_pairs",
+    )(columns.reshape(4, 4, 16, 4096)).reshape(32, 16, 16, 128)
+
+
+def from_pairs_kernel(src, dst, wide, went):
+    departures = [pltpu.make_async_copy(wide.at[k], dst.at[k], went.at[k]) for k in range(4)]
+    for k in range(4):
+        for zp in range(32):
+            wide[k, :, :, zp * 128 : (zp + 1) * 128] = src[zp, k]
+        departures[k].start()
+    for copy in departures:
+        copy.wait()
+
+
+def from_pairs(pairs):
+    return pl.pallas_call(
+        from_pairs_kernel,
+        out_shape=jax.ShapeDtypeStruct((4, 4, 16, 4096), BF16),
+        in_specs=whole(1),
+        out_specs=pl.BlockSpec(memory_space=pltpu.HBM),
+        scratch_shapes=[pltpu.VMEM((4, 4, 16, 4096), BF16), pltpu.SemaphoreType.DMA((4,))],
+        compiler_params=params(8),
+        cost_estimate=pl.CostEstimate(flops=0, bytes_accessed=4 << 20, transcendentals=0),
+        name="from_pairs",
+    )(pairs.reshape(32, 4, 4, 16, 128))
 
 
 def dft_tables(row_ids, col_ids, length):
@@ -520,8 +591,7 @@
     def exchange(values):
         return lax.all_to_all(values, axes, 0, 0, tiled=True)
 
-    cot_pairs = cotangent.reshape(16, 16, count, 128).transpose(2, 0, 1, 3)
-    cot_planes = exchange(cot_pairs).reshape(plane_shape)
+    cot_planes = exchange(to_pairs(cotangent.reshape(16, 16, 4096))).reshape(plane_shape)
 
     small = real_dft(N) + real_dft(N // 2)
     fx, ix, fy, iy, fz, iz = tables(*[jnp.asarray(v, BF16) for v in small])
@@ -538,13 +608,23 @@
     out, terms_xy = planes(first_planes, fx, ix, fy, iy, mix_x, mix_y, cot_spec, back_spec, direct)
     out_columns = exchange(out.reshape(column_shape))
 
-    grad_field, terms_z = depth_adjoint(back_columns, fz, iz, mix_z, field_spec, paired)
-    mapped = out_columns.transpose(1, 2, 0, 3).reshape(shape)
-
-    terms = jnp.concatenate([terms_xy.reshape(8, 8, N, 128), terms_z.reshape(8, 4, N, 128)], 1)
-    terms = terms.reshape(2, 2, 2, 12, 2, 2, 16, 128)
-    for dim, axis, bit in ((5, "py", 0), (4, "py", 1), (2, "px", 0), (1, "px", 1), (0, "px", 2)):
-        terms = halve(terms, dim, axis, bit)
+    def split(terms, rows):
+        return halve(terms.reshape(2, 2, 2, rows, 2, 2, 16, 128), 5, "py", 0)
+
+    terms_xy = split(terms_xy, 8)
+    terms_xy = halve(terms_xy, 4, "py", 1)
+
+    back_hat, terms_z = depth_sums(back_columns, fz, field_spec, paired)
+    mapped = from_pairs(out_columns).reshape(shape)
+
+    terms_z = split(terms_z, 4)
+    terms_z, back_hat = lax.optimization_barrier((terms_z, back_hat))
+    terms_z = halve(terms_z, 4, "py", 1)
+    grad_field = depth_adjoint(back_hat, iz, mix_z)
+    terms_z, grad_field = lax.optimization_barrier((terms_z, grad_field))
+    terms = jnp.concatenate([terms_xy, terms_z], 3)
+    for dim, bit in ((2, 0), (1, 1), (0, 2)):
+        terms = halve(terms, dim, "px", bit)
     along_z = terms[8:].reshape(4, 16, 2, C).transpose(0, 2, 1, 3).reshape(8, 16, C)
     summed = jnp.stack([terms[:8, :, :C], terms[:8, :, C:], along_z], 0)
     grad_taps = finish_taps(summed, log_part, count_py)

time: 238 us -> 226 us (0.950)
  local copies, waits for them, and re-layouts: 43.9 us -> 33.6 us
  Pallas kernels: 97.1 us -> 104 us
  waiting for transfers between devices: 56 us -> 50.7 us
  starting transfers between devices: 33 us -> 29.6 us
    pallas_call x1 -> x4, Pallas kernels: 13 us -> 20.2 us  [the longest x1 11.1 us: depth_sums(): pl.pallas_call(depth_sums_kernel, out_shape=(jax.ShapeDtypeStruct(DEPTH_S...]
    unnamed x62 -> x59, local copies, waits for them, and re-layouts: 33.2 us -> 27.1 us
    ppermute x5 -> x7, waiting for transfers between devices: 23.4 us -> 18 us  [halve(): got = lax.ppermute(send, axis, [(i, i ^ 1 << bit) for i in range(count)])]
    reshape x2 -> x0, local copies, waits for them, and re-layouts: 4.43 us -> none  [the longest x1 2.29 us: plane_device(): mapped = out_columns.transpose(1, 2, 0, 3).reshape(shape)]
    ppermute x5 -> x7, starting transfers between devices: 12.8 us -> 9.56 us  [halve(): got = lax.ppermute(send, axis, [(i, i ^ 1 << bit) for i in range(count)])]
    convert_element_type x4 -> x6, local copies, waits for them, and re-layouts: 0.13 us -> 3.33 us  [halve(): lax.dynamic_index_in_dim(values, 1 - mine, dim, keepdims=False).astype(BF16)]
    transpose x1 -> x0, local copies, waits for them, and re-layouts: 2.95 us -> none  [plane_device(): mapped = out_columns.transpose(1, 2, 0, 3).reshape(shape)]
  transfers between devices with their start and end apart: 9 -> 11, of which waited for: 7 -> 8; matrix products, arithmetic and copies ran while one was open for 8% -> 8% of each run, Pallas kernels for 41% -> 45%
where the time goes in v2:
time: 226 us; the launch traced here: 225 us
  Pallas kernels  104 us (46%)
  waiting for transfers between devices  50.7 us (22%)
  local copies, waits for them, and re-layouts  33.6 us (15%)
  starting transfers between devices  29.6 us (13%)
  other arithmetic  4.6 us (2%)
    all_to_all x4, waiting for transfers between devices, exchange(): return lax.all_to_all(values, axes, 0, 0, tiled=True)  32.8 us
    pallas_call x1, Pallas kernels, planes(): pl.pallas_call(planes_kernel, out_shape=(jax.ShapeDtypeStruct(values.shap...  30.7 us
    unnamed x59, local copies, waits for them, and re-layouts  27.1 us
    pallas_call x1, Pallas kernels, planes_adjoint(): pl.pallas_call(planes_adjoint_kernel, out_shape=(jax.ShapeDtypeStruct(val...  23.4 us
    all_to_all x4, starting transfers between devices, exchange(): return lax.all_to_all(values, axes, 0, 0, tiled=True)  20 us
    ppermute x7, waiting for transfers between devices, halve(): got = lax.ppermute(send, axis, [(i, i ^ 1 << bit) for i in range(count)])  18 us
    pallas_call x1, Pallas kernels, mixing(): pl.pallas_call(mixing_kernel, out_shape=(line, line, pair), in_specs=whol...  15 us
    pallas_call x1, Pallas kernels, depth_sums(): pl.pallas_call(depth_sums_kernel, out_shape=(jax.ShapeDtypeStruct(DEPTH_S...  11.1 us
  transfers between devices with their start and end apart: 11, of which 8 were waited for; matrix products, arithmetic and copies ran while one was open for 8% of the time, Pallas kernels for 45%

profile of v2, /device:TPU:0, one launch (start us, length us, event | category | flops | bytes accessed | tf_op | source)
XLA Modules:
  0.0 225.5 jit_solution(9023824738493585074)
XLA Ops:
  0.6 2.6 %to_pairs.1 = bf16[32,4,4,16,128]{4,3,2,1,0:T(8,128)(2,1)} custom-call(bf16[4,4,16,4096]{3,2,1,0:T(8,128)(2,1)} %bitcast.85), custom_call_target="tpu_custom_call" | custom-call | bytes 4194304 | tf_op jit(solution)/shard_map/to_pairs/pallas_call | solution.py:497
  3.3 7.5 %all-to-all-start.1 = ((bf16[32,16,16,128]{3,2,1,0:T(8,128)(2,1)}), bf16[32,16,16,128]{3,2,1,0:T(8,128)(2,1)}, u32[]{:S(2)}, u32[]{:S(2)}) async-start(bf16[32,16,16,128]{3,2,1,0:T(8,128)(2,1)} %bitcast.84), calls=%async_computation.1 | async-start | bytes 4194304 | tf_op jit(solution)/shard_map/all_to_all | solution.py:592
  10.8 15.0 %mixing.1 = (bf16[2,2,32,128,128]{4,3,2,1,0:T(8,128)(2,1)S(1)}, bf16[2,2,32,128,128]{4,3,2,1,0:T(8,128)(2,1)S(1)}, bf16[2,2,16,128,128]{4,3,2,1,0:T(8,128)(2,1)S(1)}) custom-call(bf16[3,64,64,64]{3,2,1,0:T(8,128)(2,1)S(1)} %copy-done, bf16[72,64]{1,0:T(8,128)(2,1)S(1)} %copy-done.7, bf16[128,128]{1,0:T(8,128)(2,1)S(1)} %copy-done.6), custom_call_target="tpu_custom_call" | custom-call | flops 2147483648 | bytes 12582912 | tf_op jit(solution)/shard_map/mixing/pallas_call | solution.py:208
  25.8 2.0 copy-done.17
  27.8 2.0 copy-done.18
  29.8 8.7 %tables.1 = (bf16[1024,1024]{1,0:T(8,128)(2,1)S(1)}, bf16[1024,1024]{1,0:T(8,128)(2,1)S(1)}, bf16[1024,1024]{1,0:T(8,128)(2,1)S(1)}, bf16[1024,1024]{1,0:T(8,128...) custom-call(bf16[64,64]{1,0:T(8,128)(2,1)S(1)} %copy-done.8, bf16[64,64]{1,0:T(8,128)(2,1)S(1)} %copy-done.9, ...), custom_call_target="tpu_custom_call" | custom-call | flops 2147483648 | bytes 12582912 | tf_op jit(solution)/shard_map/tables/pallas_call | solution.py:147
  38.6 1.3 copy-done.19
  39.9 1.3 copy-done.21
  41.2 1.3 copy-done.22
  42.6 1.4 copy-done.23
  43.9 6.4 %depth.1 = (bf16[32,16,16,128]{3,2,1,0:T(8,128)(2,1)S(1)}, bf16[16,16,16,256]{3,2,1,0:T(8,128)(2,1)S(1)}) custom-call(bf16[16,16,4096]{2,1,0:T(8,128)(2,1)S(1)} %bitcast.83, bf16[512,512]{1,0:T(8,128)(2,1)S(1)} %get-tuple-element.27.fwd, bf16[512,512]{1,0:T(8,128)(2,1)S(1)} %get-tuple-element.28.inv, bf16[2,2,16,128,128]{4,3,2,1,0:T(8,128)(2,1)S(1)} %get-tuple-element.29.mix), custom_call_target="tpu_custom_call" | custom-call | flops 4294967296 | bytes 10485760 | tf_op jit(solution)/shard_map/depth/pallas_call | solution.py:438
  50.4 1.3 copy-done.2
  51.7 0.8 copy-done.15
  52.5 1.3 copy-done.24
  53.8 0.8 copy-done.25
  54.6 4.9 %all-to-all-done.1 = bf16[32,16,16,128]{3,2,1,0:T(8,128)(2,1)} async-done(((bf16[32,16,16,128]{3,2,1,0:T(8,128)(2,1)}), bf16[32,16,16,128]{3,2,1,0:T(8,128)(2,1)}, u32[]{:S(2)}, u32[]{:S(2)}) %all-to-all-start.1) | async-done | bytes 2097184 | tf_op jit(solution)/shard_map/all_to_all | solution.py:592
  59.4 4.2 %all-to-all-start = ((bf16[32,16,16,128]{3,2,1,0:T(8,128)(2,1)}), bf16[32,16,16,128]{3,2,1,0:T(8,128)(2,1)}, u32[]{:S(2)}, u32[]{:S(2)}) async-start(bf16[32,16,16,128]{3,2,1,0:T(8,128)(2,1)} %copy-done.2), calls=%async_computation | async-start | bytes 4194304 | tf_op jit(solution)/shard_map/all_to_all | solution.py:592
  63.7 5.5 %copy.21 = bf16[3,64,64,64]{1,0,3,2:T(4,128)(2,1)} copy(bf16[3,64,64,64]{3,2,1,0:T(8,128)(2,1)S(1)} %copy-done) | data formatting | bytes 3145728 | tf_op args[2]
  69.1 2.9 %gather_fusion = bf16[64,3,64]{2,1,0:T(4,128)(2,1)S(1)} fusion(bf16[3,64,64,64]{1,0,3,2:T(4,128)(2,1)} %copy.21, s32[64]{0:T(128)S(1)} %or_bitcast_fusion), kind=kCustom, calls=%fused_computation | custom fusion | bytes 49664 | tf_op jit(solution)/shard_map/jit(diagonal)/gather | solution.py:545
  73.6 23.4 %planes_adjoint.1 = (bf16[8,4,2,8,16,128]{5,4,3,2,1,0:T(8,128)(2,1)}, bf16[32,8,16,256]{3,2,1,0:T(8,128)(2,1)S(1)}, bf16[32,8,16,256]{3,2,1,0:T(8,128)(2,1)S(1)}) custom-call(bf16[8,4,2,8,16,128]{5,4,3,2,1,0:T(8,128)(2,1)} %bitcast.4.values, bf16[1024,1024]{1,0:T(8,128)(2,1)} %copy-done.19, bf16[1024,1024]{1,0:T(8,128)(2,1)} %copy-done.21, ...), custom_call_target="tpu_custom_call" | custom-call | flops 10737418240 | bytes 25165824 | tf_op jit(solution)/shard_map/planes_adjoint/pallas_call | solution.py:328
  96.9 1.4 copy-done.26
  98.3 1.4 copy-done.27
  99.7 12.6 %all-to-all-done = bf16[32,16,16,128]{3,2,1,0:T(8,128)(2,1)} async-done(((bf16[32,16,16,128]{3,2,1,0:T(8,128)(2,1)}), bf16[32,16,16,128]{3,2,1,0:T(8,128)(2,1)}, u32[]{:S(2)}, u32[]{:S(2)}) %all-to-all-start) | async-done | bytes 2097184 | tf_op jit(solution)/shard_map/all_to_all | solution.py:592
  112.4 4.4 %all-to-all-start.3 = ((bf16[32,16,16,128]{3,2,1,0:T(8,128)(2,1)}), bf16[32,16,16,128]{3,2,1,0:T(8,128)(2,1)}, u32[]{:S(2)}, u32[]{:S(2)}) async-start(bf16[32,16,16,128]{3,2,1,0:T(8,128)(2,1)} %bitcast.18), calls=%async_computation.3 | async-start | bytes 4194304 | tf_op jit(solution)/shard_map/all_to_all | solution.py:592
  116.8 30.7 %planes.1 = (bf16[8,4,2,8,16,128]{5,4,3,2,1,0:T(8,128)(2,1)S(1)}, f32[4096,128]{1,0:T(8,128)S(1)}) custom-call(bf16[8,4,2,8,16,128]{5,4,3,2,1,0:T(8,128)(2,1)} %bitcast.1.values, bf16[1024,1024]{1,0:T(8,128)(2,1)S(1)} %copy-done.20, bf16[1024,1024]{1,0:T(8,128)(2,1)} %copy-done.21, bf16[1024,1024]{1,0:T(8,128)(2,1)} %copy-done.22, ...), custom_call_target="tpu_custom_call" | custom-call | flops 12884901888 | bytes 29360128 | tf_op jit(solution)/shard_map/planes/pallas_call | solution.py:345
  147.6 1.3 copy-done.1
  148.9 1.3 copy-done.3
  150.2 15.3 %all-to-all-done.3.values = bf16[32,16,16,128]{3,2,1,0:T(8,128)(2,1)} async-done(((bf16[32,16,16,128]{3,2,1,0:T(8,128)(2,1)}), bf16[32,16,16,128]{3,2,1,0:T(8,128)(2,1)}, u32[]{:S(2)}, u32[]{:S(2)}) %all-to-all-start.3) | async-done | bytes 2097184 | tf_op jit(solution)/shard_map/all_to_all | solution.py:592
  165.5 4.0 %all-to-all-start.2 = ((bf16[32,16,16,128]{3,2,1,0:T(8,128)(2,1)}), bf16[32,16,16,128]{3,2,1,0:T(8,128)(2,1)S(1)}, u32[]{:S(2)}, u32[]{:S(2)}) async-start(bf16[32,16,16,128]{3,2,1,0:T(8,128)(2,1)} %bitcast.80), calls=%async_computation.2 | async-start | bytes 4194304 | tf_op jit(solution)/shard_map/all_to_all | solution.py:592
  169.4 1.4 fusion.2
  171.1 1.7 collective-permute-done.2
  172.8 1.4 bitcast_add_fusion
  174.2 1.0 copy-done.28
  175.2 1.8 collective-permute-start.3
  177.1 11.1 %depth_sums.1 = (bf16[16,16,16,256]{3,2,1,0:T(8,128)(2,1)}, f32[2048,128]{1,0:T(8,128)}) custom-call(bf16[32,16,16,128]{3,2,1,0:T(8,128)(2,1)} %all-to-all-done.3.values, bf16[512,512]{1,0:T(8,128)(2,1)} %copy-done.25, bf16[16,16,16,256]{3,2,1,0:T(8,128)(2,1)} %copy-done.24, f32[32,64]{1,0:T(8,128)} %constant.123.clone.table), custom_call_target="tpu_custom_call" | custom-call | flops 4294967296 | bytes 8388608 | tf_op jit(solution)/shard_map/depth_sums/pallas_call | solution.py:454
  188.2 1.9 fusion.9
  190.0 1.5 collective-permute-done.3
  191.5 1.1 bitcast_add_fusion.1
  192.6 1.2 bitcast_add_fusion.2
  193.9 4.4 %collective-permute-start.1 = (bf16[2,2,2,4,16,128]{5,4,3,0,1,2:T(8,128)(2,1)S(1)}, bf16[2,2,2,4,16,128]{5,4,3,0,1,2:T(8,128)(2,1)S(1)}, u32[]{:S(2)}, u32[]{:S(2)}) collective-permute-start(bf16[2,2,2,4,16,128]{5,4,3,0,1,2:T(8,128)(2,1)S(1)} %fusion.12), channel_id=1, source_target_pairs={{0,2},{1,3},{2,0},{3,1},{4,6},{5,7},{6,4},{7,5},{8,10},{9,11},{10,... | collective-permute-start | bytes 393224 | tf_op jit(solution)/shard_map/ppermute | solution.py:578
  198.3 1.6 copy-done.14
  199.9 5.1 %depth_adjoint.1 = bf16[16,16,4096]{2,1,0:T(8,128)(2,1)} custom-call(bf16[16,16,16,256]{3,2,1,0:T(8,128)(2,1)S(1)} %copy-done.14, bf16[512,512]{1,0:T(8,128)(2,1)S(1)} %copy-done.16, bf16[2,2,16,128,128]{4,3,2,1,0:T(8,128)(2,1)S(1)} %copy-done.13), custom_call_target="tpu_custom_call" | custom-call | flops 2147483648 | bytes 6291456 | tf_op jit(solution)/shard_map/depth_adjoint/pallas_call | solution.py:470
  205.0 2.5 %collective-permute-start.4 = (bf16[2,2,12,16,128]{4,3,2,0,1:T(8,128)(2,1)S(1)}, bf16[2,2,12,16,128]{4,3,2,0,1:T(8,128)(2,1)S(1)}, u32[]{:S(2)}, u32[]{:S(2)}) collective-permute-start(bf16[2,2,12,16,128]{4,3,2,0,1:T(8,128)(2,1)S(1)} %fusion.10), channel_id=1, source_target_pairs={{0,4},{4,0},{8,12},{12,8},{16,20},{20,16},{24,28},{28,24},{1,5},{5... | collective-permute-start | bytes 589832 | tf_op jit(solution)/shard_map/ppermute | solution.py:578
  207.5 6.2 %collective-permute-done.4 = bf16[2,2,12,16,128]{4,3,2,0,1:T(8,128)(2,1)S(1)} collective-permute-done((bf16[2,2,12,16,128]{4,3,2,0,1:T(8,128)(2,1)S(1)}, bf16[2,2,12,16,128]{4,3,2,0,1:T(8,128)(2,1)S(1)}, u32[]{:S(2)}, u32[]{:S(2)}) %collective-permute-start.4) | collective-permute-done | bytes 196640 | tf_op jit(solution)/shard_map/ppermute | solution.py:578
  213.8 5.6 %collective-permute-done.5 = bf16[2,12,16,128]{3,2,1,0:T(8,128)(2,1)S(1)} collective-permute-done((bf16[2,12,16,128]{3,2,1,0:T(8,128)(2,1)S(1)}, bf16[2,12,16,128]{3,2,1,0:T(8,128)(2,1)S(1)}, u32[]{:S(2)}, u32[]{:S(2)}) %collective-permute-start.5) | collective-permute-done | bytes 98336 | tf_op jit(solution)/shard_map/ppermute | solution.py:578
  220.0 1.4 from_pairs.1
  221.5 3.0 %collective-permute-done.6 = bf16[12,16,128]{2,1,0:T(8,128)(2,1)S(1)} collective-permute-done((bf16[12,16,128]{2,1,0:T(8,128)(2,1)S(1)}, bf16[12,16,128]{2,1,0:T(8,128)(2,1)S(1)}, u32[]{:S(2)}, u32[]{:S(2)}) %collective-permute-start.6) | collective-permute-done | bytes 49184 | tf_op jit(solution)/shard_map/ppermute | solution.py:578
  224.8 0.7 fusion.11
  (70 shorter events, 3.0 us)
Async XLA Ops:
  3.2 7.5 %copy-start = (bf16[3,64,64,64]{3,2,1,0:T(8,128)(2,1)S(1)}, bf16[3,64,64,64]{3,2,1,0:T(8,128)(2,1)}, u32[]{:S(2)}) copy-start(bf16[3,64,64,64]{3,2,1,0:T(8,128)(2,1)} %taps.1) | copy-start | bytes 4718596
  3.2 7.5 %copy-start.6 = (bf16[128,128]{1,0:T(8,128)(2,1)S(1)}, bf16[128,128]{1,0:T(8,128)(2,1)}, u32[]{:S(2)}) copy-start(bf16[128,128]{1,0:T(8,128)(2,1)} %constant.121.clone.e_pair) | copy-start | bytes 98308
  3.3 7.5 %copy-start.7 = (bf16[72,64]{1,0:T(8,128)(2,1)S(1)}, bf16[72,64]{1,0:T(8,128)(2,1)}, u32[]{:S(2)}) copy-start(bf16[72,64]{1,0:T(8,128)(2,1)} %constant.120.clone.e_line) | copy-start | bytes 27652
  3.3 56.2 %all-to-all-start.1 = ((bf16[32,16,16,128]{3,2,1,0:T(8,128)(2,1)}), bf16[32,16,16,128]{3,2,1,0:T(8,128)(2,1)}, u32[]{:S(2)}, u32[]{:S(2)}) async-start(bf16[32,16,16,128]{3,2,1,0:T(8,128)(2,1)} %bitcast.84), calls=%async_computation.1 | async-start | bytes 4194304 | tf_op jit(solution)/shard_map/all_to_all | solution.py:592
  10.8 19.0 %copy-start.8 = (bf16[64,64]{1,0:T(8,128)(2,1)S(1)}, bf16[64,64]{1,0:T(8,128)(2,1)}, u32[]{:S(2)}) copy-start(bf16[64,64]{1,0:T(8,128)(2,1)} %constant.116.clone.fwd) | copy-start | bytes 24580
  10.8 19.0 %copy-start.9 = (bf16[64,64]{1,0:T(8,128)(2,1)S(1)}, bf16[64,64]{1,0:T(8,128)(2,1)}, u32[]{:S(2)}) copy-start(bf16[64,64]{1,0:T(8,128)(2,1)} %constant.117.clone.inv) | copy-start | bytes 24580
  10.8 19.0 %copy-start.10 = (bf16[32,32]{1,0:T(8,128)(2,1)S(1)}, bf16[32,32]{1,0:T(8,128)(2,1)}, u32[]{:S(2)}) copy-start(bf16[32,32]{1,0:T(8,128)(2,1)} %constant.118.clone.fwd_z) | copy-start | bytes 6148
  10.8 19.0 %copy-start.11 = (bf16[32,32]{1,0:T(8,128)(2,1)S(1)}, bf16[32,32]{1,0:T(8,128)(2,1)}, u32[]{:S(2)}) copy-start(bf16[32,32]{1,0:T(8,128)(2,1)} %constant.119.clone.inv_z) | copy-start | bytes 6148
  25.8 2.0 copy-start.17
  27.8 2.0 copy-start.18
  29.8 14.1 %copy-start.12 = (bf16[2,2,16,128,128]{4,3,2,1,0:T(8,128)(2,1)}, bf16[2,2,16,128,128]{4,3,2,1,0:T(8,128)(2,1)S(1)}, u32[]{:S(2)}) copy-start(bf16[2,2,16,128,128]{4,3,2,1,0:T(8,128)(2,1)S(1)} %get-tuple-element.29.mix) | copy-start | bytes 6291460
  29.8 14.1 %copy-start.4 = (bf16[2,8,16,4096]{3,2,1,0:T(8,128)(2,1)S(1)}, bf16[2,8,16,4096]{3,2,1,0:T(8,128)(2,1)}, u32[]{:S(2)}) copy-start(bf16[2,8,16,4096]{3,2,1,0:T(8,128)(2,1)} %param.11) | copy-start | bytes 6291460
  38.6 1.3 copy-start.19
  39.9 1.3 copy-start.21
  41.2 1.3 copy-start.22
  42.6 1.4 copy-start.23
  50.3 1.3 copy-start.2
  51.7 0.8 copy-start.15
  52.5 1.3 copy-start.24
  53.8 0.8 copy-start.25
  59.4 52.9 %all-to-all-start = ((bf16[32,16,16,128]{3,2,1,0:T(8,128)(2,1)}), bf16[32,16,16,128]{3,2,1,0:T(8,128)(2,1)}, u32[]{:S(2)}, u32[]{:S(2)}) async-start(bf16[32,16,16,128]{3,2,1,0:T(8,128)(2,1)} %copy-done.2), calls=%async_computation | async-start | bytes 4194304 | tf_op jit(solution)/shard_map/all_to_all | solution.py:592
  96.9 1.4 copy-start.26
  98.3 1.4 copy-start.27
  112.4 4.4 %copy-start.5 = (f32[64,64]{1,0:T(8,128)S(1)}, f32[64,64]{1,0:T(8,128)}, u32[]{:S(2)}) copy-start(f32[64,64]{1,0:T(8,128)} %constant.122.clone.table) | copy-start | bytes 49156
  112.4 4.4 %copy-start.20 = (bf16[1024,1024]{1,0:T(8,128)(2,1)S(1)}, bf16[1024,1024]{1,0:T(8,128)(2,1)}, u32[]{:S(2)}) copy-start(bf16[1024,1024]{1,0:T(8,128)(2,1)} %copy-done.19) | copy-start | bytes 6291460
  112.4 53.1 %all-to-all-start.3 = ((bf16[32,16,16,128]{3,2,1,0:T(8,128)(2,1)}), bf16[32,16,16,128]{3,2,1,0:T(8,128)(2,1)}, u32[]{:S(2)}, u32[]{:S(2)}) async-start(bf16[32,16,16,128]{3,2,1,0:T(8,128)(2,1)} %bitcast.18), calls=%async_computation.3 | async-start | bytes 4194304 | tf_op jit(solution)/shard_map/all_to_all | solution.py:592
  147.5 1.3 copy-start.1
  148.9 1.3 copy-start.3
  165.5 54.6 %all-to-all-start.2 = ((bf16[32,16,16,128]{3,2,1,0:T(8,128)(2,1)}), bf16[32,16,16,128]{3,2,1,0:T(8,128)(2,1)S(1)}, u32[]{:S(2)}, u32[]{:S(2)}) async-start(bf16[32,16,16,128]{3,2,1,0:T(8,128)(2,1)} %bitcast.80), calls=%async_computation.2 | async-start | bytes 4194304 | tf_op jit(solution)/shard_map/all_to_all | solution.py:592
  170.8 2.0 collective-permute-start.2
  174.1 1.0 copy-start.28
  175.2 16.3 %collective-permute-start.3 = (bf16[2,2,2,8,16,128]{5,4,3,0,1,2:T(8,128)(2,1)S(1)}, bf16[2,2,2,8,16,128]{5,4,3,0,1,2:T(8,128)(2,1)S(1)}, u32[]{:S(2)}, u32[]{:S(2)}) collective-permute-start(bf16[2,2,2,8,16,128]{5,4,3,0,1,2:T(8,128)(2,1)S(1)} %fusion.8), channel_id=1, source_target_pairs={{0,2},{1,3},{2,0},{3,1},{4,6},{5,7},{6,4},{7,5},{8,10},{9,11},{10,... | collective-permute-start | bytes 786440 | tf_op jit(solution)/shard_map/ppermute | solution.py:578
  188.2 10.1 %copy-start.16 = (bf16[512,512]{1,0:T(8,128)(2,1)S(1)}, bf16[512,512]{1,0:T(8,128)(2,1)}, u32[]{:S(2)}) copy-start(bf16[512,512]{1,0:T(8,128)(2,1)} %copy-done.15) | copy-start | bytes 1572868
  190.0 2.6 %collective-permute-start = (bf16[2,2,2,4,2,16,128]{6,5,3,0,1,2,4:T(8,128)(2,1)}, bf16[2,2,2,4,2,16,128]{6,5,3,0,1,2,4:T(8,128)(2,1)}, u32[]{:S(2)}, u32[]{:S(2)}) collective-permute-start(bf16[2,2,2,4,2,16,128]{6,5,3,0,1,2,4:T(8,128)(2,1)} %fusion.9), channel_id=1, source_target_pairs={{0,1},{1,0},{2,3},{3,2},{4,5},{5,4},{6,7},{7,6},{8,9},{9,8},{10,11... | collective-permute-start | bytes 786440 | tf_op jit(solution)/shard_map/ppermute | solution.py:578
  190.0 8.2 %copy-start.13 = (bf16[2,2,16,128,128]{4,3,2,1,0:T(8,128)(2,1)S(1)}, bf16[2,2,16,128,128]{4,3,2,1,0:T(8,128)(2,1)}, u32[]{:S(2)}) copy-start(bf16[2,2,16,128,128]{4,3,2,1,0:T(8,128)(2,1)} %copy-done.12) | copy-start | bytes 6291460
  193.9 11.0 %collective-permute-start.1 = (bf16[2,2,2,4,16,128]{5,4,3,0,1,2:T(8,128)(2,1)S(1)}, bf16[2,2,2,4,16,128]{5,4,3,0,1,2:T(8,128)(2,1)S(1)}, u32[]{:S(2)}, u32[]{:S(2)}) collective-permute-start(bf16[2,2,2,4,16,128]{5,4,3,0,1,2:T(8,128)(2,1)S(1)} %fusion.12), channel_id=1, source_target_pairs={{0,2},{1,3},{2,0},{3,1},{4,6},{5,7},{6,4},{7,5},{8,10},{9,11},{10,... | collective-permute-start | bytes 393224 | tf_op jit(solution)/shard_map/ppermute | solution.py:578
  198.3 1.6 copy-start.14
  205.0 8.6 %collective-permute-start.4 = (bf16[2,2,12,16,128]{4,3,2,0,1:T(8,128)(2,1)S(1)}, bf16[2,2,12,16,128]{4,3,2,0,1:T(8,128)(2,1)S(1)}, u32[]{:S(2)}, u32[]{:S(2)}) collective-permute-start(bf16[2,2,12,16,128]{4,3,2,0,1:T(8,128)(2,1)S(1)} %fusion.10), channel_id=1, source_target_pairs={{0,4},{4,0},{8,12},{12,8},{16,20},{20,16},{24,28},{28,24},{1,5},{5... | collective-permute-start | bytes 589832 | tf_op jit(solution)/shard_map/ppermute | solution.py:578
  213.7 5.7 %collective-permute-start.5 = (bf16[2,12,16,128]{3,2,1,0:T(8,128)(2,1)S(1)}, bf16[2,12,16,128]{3,2,1,0:T(8,128)(2,1)S(1)}, u32[]{:S(2)}, u32[]{:S(2)}) collective-permute-start(bf16[2,12,16,128]{3,2,1,0:T(8,128)(2,1)S(1)} %fusion.13), channel_id=1, source_target_pairs={{0,8},{4,12},{8,0},{12,4},{16,24},{20,28},{24,16},{28,20},{1,9},{5... | collective-permute-start | bytes 294920 | tf_op jit(solution)/shard_map/ppermute | solution.py:578
  219.5 5.1 %collective-permute-start.6 = (bf16[12,16,128]{2,1,0:T(8,128)(2,1)S(1)}, bf16[12,16,128]{2,1,0:T(8,128)(2,1)S(1)}, u32[]{:S(2)}, u32[]{:S(2)}) collective-permute-start(bf16[12,16,128]{2,1,0:T(8,128)(2,1)S(1)} %fusion.18), channel_id=1, source_target_pairs={{0,16},{4,20},{8,24},{12,28},{16,0},{20,4},{24,8},{28,12},{1,17},{... | collective-permute-start | bytes 147464 | tf_op jit(solution)/shard_map/ppermute | solution.py:578

commit v3 on v2

--- a/solution.py
+++ b/solution.py
@@ -511,27 +511,47 @@
     )(columns.reshape(4, 4, 16, 4096)).reshape(32, 16, 16, 128)
 
 
-def from_pairs_kernel(src, dst, wide, went):
+def last_kernel(src, kept, got, mask, log_rows, dst, taps_dst, wide, lags, went, done):
     departures = [pltpu.make_async_copy(wide.at[k], dst.at[k], went.at[k]) for k in range(4)]
     for k in range(4):
         for zp in range(32):
             wide[k, :, :, zp * 128 : (zp + 1) * 128] = src[zp, k]
         departures[k].start()
+    inside = mask[...]
+    for row in range(12):
+        sums = kept[row] + got[row].astype(F32)
+        other = pltpu.roll(sums, 64, 1)
+        for half in range(2):
+            axis, lag = (half, row) if row < 8 else (2, 2 * (row - 8) + half)
+            value = (other if half else sums)[:, :64]
+            lags[axis, lag] = inside * value - log_rows[axis, lag]
+    taps_copy = pltpu.make_async_copy(lags, taps_dst, done)
+    taps_copy.start()
     for copy in departures:
         copy.wait()
-
-
-def from_pairs(pairs):
+    taps_copy.wait()
+
+
+def last_stage(pairs, kept, got, mask, log_rows):
+    hbm = pl.BlockSpec(memory_space=pltpu.HBM)
     return pl.pallas_call(
-        from_pairs_kernel,
-        out_shape=jax.ShapeDtypeStruct((4, 4, 16, 4096), BF16),
-        in_specs=whole(1),
-        out_specs=pl.BlockSpec(memory_space=pltpu.HBM),
-        scratch_shapes=[pltpu.VMEM((4, 4, 16, 4096), BF16), pltpu.SemaphoreType.DMA((4,))],
+        last_kernel,
+        out_shape=(
+            jax.ShapeDtypeStruct((4, 4, 16, 4096), BF16),
+            jax.ShapeDtypeStruct((3, 8, 16, 64), F32),
+        ),
+        in_specs=whole(5),
+        out_specs=(hbm, hbm),
+        scratch_shapes=[
+            pltpu.VMEM((4, 4, 16, 4096), BF16),
+            pltpu.VMEM((3, 8, 16, 64), F32),
+            pltpu.SemaphoreType.DMA((4,)),
+            pltpu.SemaphoreType.DMA,
+        ],
         compiler_params=params(8),
         cost_estimate=pl.CostEstimate(flops=0, bytes_accessed=4 << 20, transcendentals=0),
-        name="from_pairs",
-    )(pairs.reshape(32, 4, 4, 16, 128))
+        name="last_stage",
+    )(pairs.reshape(32, 4, 4, 16, 128), kept, got, mask, log_rows)
 
 
 def dft_tables(row_ids, col_ids, length):
@@ -570,12 +590,17 @@
     return keep_mask * (summed - log_part[:, :, None, :] * diagonal_sel)
 
 
-def halve(values, dim, axis, bit):
+def halve_parts(values, dim, axis, bit):
     count = lax.axis_size(axis)
     mine = (lax.axis_index(axis) >> bit) & 1
     keep = lax.dynamic_index_in_dim(values, mine, dim, keepdims=False)
     send = lax.dynamic_index_in_dim(values, 1 - mine, dim, keepdims=False).astype(BF16)
     got = lax.ppermute(send, axis, [(i, i ^ (1 << bit)) for i in range(count)])
+    return keep, got
+
+
+def halve(values, dim, axis, bit):
+    keep, got = halve_parts(values, dim, axis, bit)
     return keep + got.astype(F32)
 
 
@@ -601,7 +626,10 @@
     first, field_spec = depth(field.reshape(16, 16, 4096), fz, iz, mix_z)
     first_planes = exchange(first).reshape(plane_shape)
 
-    fx_then, log_part = lax.optimization_barrier((fx, own_log_terms(taps, count_px)))
+    own_rows = lax.axis_index("py") * 16 + jnp.arange(16, dtype=jnp.int32)
+    diagonal = (jnp.arange(C, dtype=jnp.int32)[None, :] == own_rows[:, None]).astype(F32)
+    log_rows = own_log_terms(taps, count_px)[:, :, None, :] * diagonal
+    fx_then, log_rows = lax.optimization_barrier((fx, log_rows))
     back_one, cot_spec, back_spec = planes_adjoint(cot_planes, fx_then, ix, fy, iy, mix_x, mix_y)
     back_columns = exchange(back_one.reshape(column_shape))
 
@@ -615,20 +643,20 @@
     terms_xy = halve(terms_xy, 4, "py", 1)
 
     back_hat, terms_z = depth_sums(back_columns, fz, field_spec, paired)
-    mapped = from_pairs(out_columns).reshape(shape)
 
     terms_z = split(terms_z, 4)
+    terms_z = halve(terms_z, 4, "py", 1)
     terms_z, back_hat = lax.optimization_barrier((terms_z, back_hat))
-    terms_z = halve(terms_z, 4, "py", 1)
+    terms = halve(jnp.concatenate([terms_xy, terms_z], 3), 2, "px", 0)
     grad_field = depth_adjoint(back_hat, iz, mix_z)
-    terms_z, grad_field = lax.optimization_barrier((terms_z, grad_field))
-    terms = jnp.concatenate([terms_xy, terms_z], 3)
-    for dim, bit in ((2, 0), (1, 1), (0, 2)):
-        terms = halve(terms, dim, "px", bit)
-    along_z = terms[8:].reshape(4, 16, 2, C).transpose(0, 2, 1, 3).reshape(8, 16, C)
-    summed = jnp.stack([terms[:8, :, :C], terms[:8, :, C:], along_z], 0)
-    grad_taps = finish_taps(summed, log_part, count_py)
-    return (mapped, grad_field.reshape(shape), grad_taps)
+    terms, grad_field = lax.optimization_barrier((terms, grad_field))
+    terms = halve(terms, 1, "px", 1)
+    kept, got = halve_parts(terms, 0, "px", 2)
+    o_ids = lax.axis_index("py") * 16 + jnp.arange(16, dtype=jnp.int32)
+    channel_ids = jnp.arange(C, dtype=jnp.int32)
+    inside = (channel_ids[None, :] <= o_ids[:, None]).astype(F32)
+    mapped, grad_taps = last_stage(out_columns, kept, got, inside, log_rows)
+    return (mapped.reshape(shape), grad_field.reshape(shape), grad_taps)
 
 
 def along(values, table, position):

time: 226 us -> 223 us (0.987)
  waiting for transfers between devices: 50.7 us -> 57.7 us
  other arithmetic: 4.6 us -> 0.56 us
  local copies, waits for them, and re-layouts: 33.6 us -> 30.2 us
  starting transfers between devices: 29.6 us -> 27 us
    ppermute x7, waiting for transfers between devices: 18 us -> 22.2 us  [halve_parts(): got = lax.ppermute(send, axis, [(i, i ^ 1 << bit) for i in range(count)])]
    add x7 -> x6, other arithmetic: 3.76 us -> 0.41 us  [halve(): return keep + got.astype(F32)]
    all_to_all x4, waiting for transfers between devices: 32.8 us -> 35.4 us  [exchange(): return lax.all_to_all(values, axes, 0, 0, tiled=True)]
    unnamed x59 -> x61, local copies, waits for them, and re-layouts: 27.1 us -> 24.6 us
    ppermute x7, starting transfers between devices: 9.56 us -> 6.99 us  [halve_parts(): got = lax.ppermute(send, axis, [(i, i ^ 1 << bit) for i in range(count)])]
  transfers between devices with their start and end apart: 11 -> 11, of which waited for: 8 -> 9; matrix products, arithmetic and copies ran while one was open for 8% -> 6% of each run, Pallas kernels for 45% -> 45%
where the time goes in v3:
time: 223 us
  Pallas kernels  105 us (47%)
  waiting for transfers between devices  57.7 us (26%)
  local copies, waits for them, and re-layouts  30.2 us (14%)
  starting transfers between devices  27 us (12%)
    all_to_all x4, waiting for transfers between devices, exchange(): return lax.all_to_all(values, axes, 0, 0, tiled=True)  35.4 us
    pallas_call x1, Pallas kernels, planes(): pl.pallas_call(planes_kernel, out_shape=(jax.ShapeDtypeStruct(values.shap...  30.7 us
    unnamed x61, local copies, waits for them, and re-layouts  24.6 us
    pallas_call x1, Pallas kernels, planes_adjoint(): pl.pallas_call(planes_adjoint_kernel, out_shape=(jax.ShapeDtypeStruct(val...  23.4 us
    ppermute x7, waiting for transfers between devices, halve_parts(): got = lax.ppermute(send, axis, [(i, i ^ 1 << bit) for i in range(count)])  22.2 us
    all_to_all x4, starting transfers between devices, exchange(): return lax.all_to_all(values, axes, 0, 0, tiled=True)  20 us
    pallas_call x1, Pallas kernels, mixing(): pl.pallas_call(mixing_kernel, out_shape=(line, line, pair), in_specs=whol...  15 us
    pallas_call x1, Pallas kernels, depth_sums(): pl.pallas_call(depth_sums_kernel, out_shape=(jax.ShapeDtypeStruct(DEPTH_S...  11.4 us
  transfers between devices with their start and end apart: 11, of which 9 were waited for; matrix products, arithmetic and copies ran while one was open for 6% of the time, Pallas kernels for 45%

profile of v3, /device:TPU:0, one launch (start us, length us, event | category | flops | bytes accessed | tf_op | source)
XLA Modules:
  0.0 222.9 jit_solution(580493871869524320)
XLA Ops:
  0.6 2.6 %to_pairs.1 = bf16[32,4,4,16,128]{4,3,2,1,0:T(8,128)(2,1)} custom-call(bf16[4,4,16,4096]{3,2,1,0:T(8,128)(2,1)} %bitcast.78), custom_call_target="tpu_custom_call" | custom-call | bytes 4194304 | tf_op jit(solution)/shard_map/to_pairs/pallas_call | solution.py:497
  3.3 7.5 %all-to-all-start.1 = ((bf16[32,16,16,128]{3,2,1,0:T(8,128)(2,1)}), bf16[32,16,16,128]{3,2,1,0:T(8,128)(2,1)}, u32[]{:S(2)}, u32[]{:S(2)}) async-start(bf16[32,16,16,128]{3,2,1,0:T(8,128)(2,1)} %bitcast.77), calls=%async_computation.1 | async-start | bytes 4194304 | tf_op jit(solution)/shard_map/all_to_all | solution.py:617
  10.8 15.0 %mixing.1 = (bf16[2,2,32,128,128]{4,3,2,1,0:T(8,128)(2,1)S(1)}, bf16[2,2,32,128,128]{4,3,2,1,0:T(8,128)(2,1)S(1)}, bf16[2,2,16,128,128]{4,3,2,1,0:T(8,128)(2,1)S(1)}) custom-call(bf16[3,64,64,64]{3,2,1,0:T(8,128)(2,1)S(1)} %copy-done, bf16[72,64]{1,0:T(8,128)(2,1)S(1)} %copy-done.8, bf16[128,128]{1,0:T(8,128)(2,1)S(1)} %copy-done.7), custom_call_target="tpu_custom_call" | custom-call | flops 2147483648 | bytes 12582912 | tf_op jit(solution)/shard_map/mixing/pallas_call | solution.py:208
  25.8 2.0 copy-done.18
  27.8 2.0 copy-done.19
  29.9 8.7 %tables.1 = (bf16[1024,1024]{1,0:T(8,128)(2,1)S(1)}, bf16[1024,1024]{1,0:T(8,128)(2,1)S(1)}, bf16[1024,1024]{1,0:T(8,128)(2,1)S(1)}, bf16[1024,1024]{1,0:T(8,128...) custom-call(bf16[64,64]{1,0:T(8,128)(2,1)S(1)} %copy-done.9, bf16[64,64]{1,0:T(8,128)(2,1)S(1)} %copy-done.10, ...), custom_call_target="tpu_custom_call" | custom-call | flops 2147483648 | bytes 12582912 | tf_op jit(solution)/shard_map/tables/pallas_call | solution.py:147
  38.6 1.3 copy-done.20
  39.9 1.3 copy-done.22
  41.2 1.3 copy-done.23
  42.6 1.4 copy-done.24
  43.9 6.4 %depth.1 = (bf16[32,16,16,128]{3,2,1,0:T(8,128)(2,1)S(1)}, bf16[16,16,16,256]{3,2,1,0:T(8,128)(2,1)S(1)}) custom-call(bf16[16,16,4096]{2,1,0:T(8,128)(2,1)S(1)} %bitcast.76, bf16[512,512]{1,0:T(8,128)(2,1)S(1)} %get-tuple-element.29.fwd, bf16[512,512]{1,0:T(8,128)(2,1)S(1)} %get-tuple-element.30.inv, bf16[2,2,16,128,128]{4,3,2,1,0:T(8,128)(2,1)S(1)} %get-tuple-element.31.mix), custom_call_target="tpu_custom_call" | custom-call | flops 4294967296 | bytes 10485760 | tf_op jit(solution)/shard_map/depth/pallas_call | solution.py:438
  50.4 1.3 copy-done.2
  51.7 0.8 copy-done.16
  52.5 1.3 copy-done.25
  53.8 0.8 copy-done.26
  54.6 4.9 %all-to-all-done.1 = bf16[32,16,16,128]{3,2,1,0:T(8,128)(2,1)} async-done(((bf16[32,16,16,128]{3,2,1,0:T(8,128)(2,1)}), bf16[32,16,16,128]{3,2,1,0:T(8,128)(2,1)}, u32[]{:S(2)}, u32[]{:S(2)}) %all-to-all-start.1) | async-done | bytes 2097184 | tf_op jit(solution)/shard_map/all_to_all | solution.py:617
  59.5 4.2 %all-to-all-start = ((bf16[32,16,16,128]{3,2,1,0:T(8,128)(2,1)}), bf16[32,16,16,128]{3,2,1,0:T(8,128)(2,1)}, u32[]{:S(2)}, u32[]{:S(2)}) async-start(bf16[32,16,16,128]{3,2,1,0:T(8,128)(2,1)} %copy-done.2), calls=%async_computation | async-start | bytes 4194304 | tf_op jit(solution)/shard_map/all_to_all | solution.py:617
  63.7 5.5 %copy.16 = bf16[3,64,64,64]{1,0,3,2:T(4,128)(2,1)} copy(bf16[3,64,64,64]{3,2,1,0:T(8,128)(2,1)S(1)} %copy-done) | data formatting | bytes 3145728 | tf_op args[2]
  69.2 2.9 %gather_fusion = bf16[64,3,64]{2,1,0:T(4,128)(2,1)S(1)} fusion(bf16[3,64,64,64]{1,0,3,2:T(4,128)(2,1)} %copy.16, s32[64]{0:T(128)S(1)} %or_bitcast_fusion), kind=kCustom, calls=%fused_computation | custom fusion | bytes 49664 | tf_op jit(solution)/shard_map/jit(diagonal)/gather | solution.py:565
  72.2 0.3 convolution_bitcast_fusion
  72.6 0.3 fusion.18
  72.9 0.3 fusion.15
  73.2 0.4 fusion.1
  73.7 23.4 %planes_adjoint.1 = (bf16[8,4,2,8,16,128]{5,4,3,2,1,0:T(8,128)(2,1)}, bf16[32,8,16,256]{3,2,1,0:T(8,128)(2,1)S(1)}, bf16[32,8,16,256]{3,2,1,0:T(8,128)(2,1)S(1)}) custom-call(bf16[8,4,2,8,16,128]{5,4,3,2,1,0:T(8,128)(2,1)} %bitcast.4.values, bf16[1024,1024]{1,0:T(8,128)(2,1)} %copy-done.20, bf16[1024,1024]{1,0:T(8,128)(2,1)} %copy-done.22, ...), custom_call_target="tpu_custom_call" | custom-call | flops 10737418240 | bytes 25165824 | tf_op jit(solution)/shard_map/planes_adjoint/pallas_call | solution.py:328
  97.1 1.4 copy-done.27
  98.5 1.4 copy-done.28
  99.9 12.5 %all-to-all-done = bf16[32,16,16,128]{3,2,1,0:T(8,128)(2,1)} async-done(((bf16[32,16,16,128]{3,2,1,0:T(8,128)(2,1)}), bf16[32,16,16,128]{3,2,1,0:T(8,128)(2,1)}, u32[]{:S(2)}, u32[]{:S(2)}) %all-to-all-start) | async-done | bytes 2097184 | tf_op jit(solution)/shard_map/all_to_all | solution.py:617
  112.4 4.4 %all-to-all-start.3 = ((bf16[32,16,16,128]{3,2,1,0:T(8,128)(2,1)}), bf16[32,16,16,128]{3,2,1,0:T(8,128)(2,1)}, u32[]{:S(2)}, u32[]{:S(2)}) async-start(bf16[32,16,16,128]{3,2,1,0:T(8,128)(2,1)} %bitcast.22), calls=%async_computation.3 | async-start | bytes 4194304 | tf_op jit(solution)/shard_map/all_to_all | solution.py:617
  116.8 30.7 %planes.1 = (bf16[8,4,2,8,16,128]{5,4,3,2,1,0:T(8,128)(2,1)S(1)}, f32[4096,128]{1,0:T(8,128)S(1)}) custom-call(bf16[8,4,2,8,16,128]{5,4,3,2,1,0:T(8,128)(2,1)} %bitcast.1.values, bf16[1024,1024]{1,0:T(8,128)(2,1)S(1)} %copy-done.21, bf16[1024,1024]{1,0:T(8,128)(2,1)} %copy-done.22, bf16[1024,1024]{1,0:T(8,128)(2,1)} %copy-done.23, ...), custom_call_target="tpu_custom_call" | custom-call | flops 12884901888 | bytes 29360128 | tf_op jit(solution)/shard_map/planes/pallas_call | solution.py:345
  147.6 1.3 copy-done.1
  148.9 1.3 copy-done.3
  150.2 15.3 %all-to-all-done.3.values = bf16[32,16,16,128]{3,2,1,0:T(8,128)(2,1)} async-done(((bf16[32,16,16,128]{3,2,1,0:T(8,128)(2,1)}), bf16[32,16,16,128]{3,2,1,0:T(8,128)(2,1)}, u32[]{:S(2)}, u32[]{:S(2)}) %all-to-all-start.3) | async-done | bytes 2097184 | tf_op jit(solution)/shard_map/all_to_all | solution.py:617
  165.5 4.0 %all-to-all-start.2 = ((bf16[32,16,16,128]{3,2,1,0:T(8,128)(2,1)}), bf16[32,16,16,128]{3,2,1,0:T(8,128)(2,1)S(1)}, u32[]{:S(2)}, u32[]{:S(2)}) async-start(bf16[32,16,16,128]{3,2,1,0:T(8,128)(2,1)} %bitcast.73), calls=%async_computation.2 | async-start | bytes 4194304 | tf_op jit(solution)/shard_map/all_to_all | solution.py:617
  169.4 1.4 fusion.2
  171.1 11.4 %depth_sums.1 = (bf16[16,16,16,256]{3,2,1,0:T(8,128)(2,1)}, f32[2048,128]{1,0:T(8,128)}) custom-call(bf16[32,16,16,128]{3,2,1,0:T(8,128)(2,1)} %all-to-all-done.3.values, bf16[512,512]{1,0:T(8,128)(2,1)} %copy-done.26, bf16[16,16,16,256]{3,2,1,0:T(8,128)(2,1)} %copy-done.25, f32[32,64]{1,0:T(8,128)} %constant.123.clone.table), custom_call_target="tpu_custom_call" | custom-call | flops 4294967296 | bytes 8388608 | tf_op jit(solution)/shard_map/depth_sums/pallas_call | solution.py:454
  182.5 1.2 fusion.9
  184.3 1.8 collective-permute-start.1
  186.3 0.9 collective-permute-start.3
  187.2 13.0 %collective-permute-done.1 = bf16[2,2,2,8,16,128]{5,4,3,0,1,2:T(8,128)(2,1)S(1)} collective-permute-done((bf16[2,2,2,8,16,128]{5,4,3,0,1,2:T(8,128)(2,1)S(1)}, bf16[2,2,2,8,16,128]{5,4,3,0,1,2:T(8,128)(2,1)S(1)}, u32[]{:S(2)}, u32[]{:S(2)}) %collective-permute-start.1) | collective-permute-done | bytes 262176 | tf_op jit(solution)/shard_map/ppermute | solution.py:598
  200.2 2.2 collective-permute-done.3
  202.5 1.6 collective-permute-start.4
  204.1 5.0 %depth_adjoint.1 = bf16[16,16,4096]{2,1,0:T(8,128)(2,1)} custom-call(bf16[16,16,16,256]{3,2,1,0:T(8,128)(2,1)S(1)} %copy-done.15, bf16[512,512]{1,0:T(8,128)(2,1)S(1)} %copy-done.17, bf16[2,2,16,128,128]{4,3,2,1,0:T(8,128)(2,1)S(1)} %copy-done.14), custom_call_target="tpu_custom_call" | custom-call | flops 2147483648 | bytes 6291456 | tf_op jit(solution)/shard_map/depth_adjoint/pallas_call | solution.py:470
  209.2 1.4 collective-permute-done.4
  210.6 1.9 collective-permute-start.5
  212.5 3.5 %collective-permute-done.5 = bf16[2,12,16,128]{3,2,1,0:T(8,128)(2,1)S(1)} collective-permute-done((bf16[2,12,16,128]{3,2,1,0:T(8,128)(2,1)S(1)}, bf16[2,12,16,128]{3,2,1,0:T(8,128)(2,1)S(1)}, u32[]{:S(2)}, u32[]{:S(2)}) %collective-permute-start.5) | collective-permute-done | bytes 98336 | tf_op jit(solution)/shard_map/ppermute | solution.py:598
  216.2 2.8 %all-to-all-done.2 = bf16[32,16,16,128]{3,2,1,0:T(8,128)(2,1)S(1)} async-done(((bf16[32,16,16,128]{3,2,1,0:T(8,128)(2,1)}), bf16[32,16,16,128]{3,2,1,0:T(8,128)(2,1)S(1)}, u32[]{:S(2)}, u32[]{:S(2)}) %all-to-all-start.2) | async-done | bytes 2097184 | tf_op jit(solution)/shard_map/all_to_all | solution.py:617
  219.0 2.2 collective-permute-done.6.got
  221.2 1.5 last_stage.1
  (68 shorter events, 1.5 us)
Async XLA Ops:
  3.2 7.5 %copy-start = (bf16[3,64,64,64]{3,2,1,0:T(8,128)(2,1)S(1)}, bf16[3,64,64,64]{3,2,1,0:T(8,128)(2,1)}, u32[]{:S(2)}) copy-start(bf16[3,64,64,64]{3,2,1,0:T(8,128)(2,1)} %taps.1) | copy-start | bytes 4718596
  3.3 7.5 %copy-start.7 = (bf16[128,128]{1,0:T(8,128)(2,1)S(1)}, bf16[128,128]{1,0:T(8,128)(2,1)}, u32[]{:S(2)}) copy-start(bf16[128,128]{1,0:T(8,128)(2,1)} %constant.121.clone.e_pair) | copy-start | bytes 98308
  3.3 7.5 %copy-start.8 = (bf16[72,64]{1,0:T(8,128)(2,1)S(1)}, bf16[72,64]{1,0:T(8,128)(2,1)}, u32[]{:S(2)}) copy-start(bf16[72,64]{1,0:T(8,128)(2,1)} %constant.120.clone.e_line) | copy-start | bytes 27652
  3.3 56.2 %all-to-all-start.1 = ((bf16[32,16,16,128]{3,2,1,0:T(8,128)(2,1)}), bf16[32,16,16,128]{3,2,1,0:T(8,128)(2,1)}, u32[]{:S(2)}, u32[]{:S(2)}) async-start(bf16[32,16,16,128]{3,2,1,0:T(8,128)(2,1)} %bitcast.77), calls=%async_computation.1 | async-start | bytes 4194304 | tf_op jit(solution)/shard_map/all_to_all | solution.py:617
  10.8 19.0 %copy-start.9 = (bf16[64,64]{1,0:T(8,128)(2,1)S(1)}, bf16[64,64]{1,0:T(8,128)(2,1)}, u32[]{:S(2)}) copy-start(bf16[64,64]{1,0:T(8,128)(2,1)} %constant.116.clone.fwd) | copy-start | bytes 24580
  10.8 19.0 %copy-start.10 = (bf16[64,64]{1,0:T(8,128)(2,1)S(1)}, bf16[64,64]{1,0:T(8,128)(2,1)}, u32[]{:S(2)}) copy-start(bf16[64,64]{1,0:T(8,128)(2,1)} %constant.117.clone.inv) | copy-start | bytes 24580
  10.8 19.0 %copy-start.11 = (bf16[32,32]{1,0:T(8,128)(2,1)S(1)}, bf16[32,32]{1,0:T(8,128)(2,1)}, u32[]{:S(2)}) copy-start(bf16[32,32]{1,0:T(8,128)(2,1)} %constant.118.clone.fwd_z) | copy-start | bytes 6148
  10.8 19.0 %copy-start.12 = (bf16[32,32]{1,0:T(8,128)(2,1)S(1)}, bf16[32,32]{1,0:T(8,128)(2,1)}, u32[]{:S(2)}) copy-start(bf16[32,32]{1,0:T(8,128)(2,1)} %constant.119.clone.inv_z) | copy-start | bytes 6148
  25.8 2.0 copy-start.18
  27.8 2.0 copy-start.19
  29.8 14.1 %copy-start.13 = (bf16[2,2,16,128,128]{4,3,2,1,0:T(8,128)(2,1)}, bf16[2,2,16,128,128]{4,3,2,1,0:T(8,128)(2,1)S(1)}, u32[]{:S(2)}) copy-start(bf16[2,2,16,128,128]{4,3,2,1,0:T(8,128)(2,1)S(1)} %get-tuple-element.31.mix) | copy-start | bytes 6291460
  29.8 14.1 %copy-start.5 = (bf16[2,8,16,4096]{3,2,1,0:T(8,128)(2,1)S(1)}, bf16[2,8,16,4096]{3,2,1,0:T(8,128)(2,1)}, u32[]{:S(2)}) copy-start(bf16[2,8,16,4096]{3,2,1,0:T(8,128)(2,1)} %param.11) | copy-start | bytes 6291460
  38.6 1.3 copy-start.20
  39.9 1.3 copy-start.22
  41.2 1.3 copy-start.23
  42.6 1.4 copy-start.24
  50.3 1.3 copy-start.2
  51.7 0.8 copy-start.16
  52.5 1.3 copy-start.25
  53.8 0.8 copy-start.26
  59.5 52.9 %all-to-all-start = ((bf16[32,16,16,128]{3,2,1,0:T(8,128)(2,1)}), bf16[32,16,16,128]{3,2,1,0:T(8,128)(2,1)}, u32[]{:S(2)}, u32[]{:S(2)}) async-start(bf16[32,16,16,128]{3,2,1,0:T(8,128)(2,1)} %copy-done.2), calls=%async_computation | async-start | bytes 4194304 | tf_op jit(solution)/shard_map/all_to_all | solution.py:617
  97.1 1.4 copy-start.27
  98.5 1.4 copy-start.28
  112.4 4.4 %copy-start.6 = (f32[64,64]{1,0:T(8,128)S(1)}, f32[64,64]{1,0:T(8,128)}, u32[]{:S(2)}) copy-start(f32[64,64]{1,0:T(8,128)} %constant.122.clone.table) | copy-start | bytes 49156
  112.4 4.4 %copy-start.21 = (bf16[1024,1024]{1,0:T(8,128)(2,1)S(1)}, bf16[1024,1024]{1,0:T(8,128)(2,1)}, u32[]{:S(2)}) copy-start(bf16[1024,1024]{1,0:T(8,128)(2,1)} %copy-done.20) | copy-start | bytes 6291460
  112.4 53.1 %all-to-all-start.3 = ((bf16[32,16,16,128]{3,2,1,0:T(8,128)(2,1)}), bf16[32,16,16,128]{3,2,1,0:T(8,128)(2,1)}, u32[]{:S(2)}, u32[]{:S(2)}) async-start(bf16[32,16,16,128]{3,2,1,0:T(8,128)(2,1)} %bitcast.22), calls=%async_computation.3 | async-start | bytes 4194304 | tf_op jit(solution)/shard_map/all_to_all | solution.py:617
  147.6 1.3 copy-start.1
  148.9 1.3 copy-start.3
  165.5 53.5 %all-to-all-start.2 = ((bf16[32,16,16,128]{3,2,1,0:T(8,128)(2,1)}), bf16[32,16,16,128]{3,2,1,0:T(8,128)(2,1)S(1)}, u32[]{:S(2)}, u32[]{:S(2)}) async-start(bf16[32,16,16,128]{3,2,1,0:T(8,128)(2,1)} %bitcast.73), calls=%async_computation.2 | async-start | bytes 4194304 | tf_op jit(solution)/shard_map/all_to_all | solution.py:617
  170.8 13.2 %collective-permute-start = (bf16[2,2,2,8,2,16,128]{6,5,3,0,1,2,4:T(8,128)(2,1)S(1)}, bf16[2,2,2,8,2,16,128]{6,5,3,0,1,2,4:T(8,128)(2,1)S(1)}, u32[]{:S(2)}, u32[]{:S(2)}) collective-permute-start(bf16[2,2,2,8,2,16,128]{6,5,3,0,1,2,4:T(8,128)(2,1)S(1)} %fusion.2), channel_id=1, source_target_pairs={{0,1},{1,0},{2,3},{3,2},{4,5},{5,4},{6,7},{7,6},{8,9},{9,8},{10,11... | collective-permute-start | bytes 1572872 | tf_op jit(solution)/shard_map/ppermute | solution.py:598
  171.1 12.9 %copy-start.4 = (f32[4096,128]{1,0:T(8,128)S(1)}, f32[4096,128]{1,0:T(8,128)}, u32[]{:S(2)}) copy-start(f32[4096,128]{1,0:T(8,128)} %copy-done.3) | copy-start | bytes 6291460
  182.5 3.7 %copy-start.29 = (f32[2048,128]{1,0:T(8,128)S(1)}, f32[2048,128]{1,0:T(8,128)}, u32[]{:S(2)}) copy-start(f32[2048,128]{1,0:T(8,128)} %get-tuple-element.46) | copy-start | bytes 3145732
  183.7 2.5 %collective-permute-start.2 = (bf16[2,2,2,4,2,16,128]{6,5,3,0,1,2,4:T(8,128)(2,1)S(1)}, bf16[2,2,2,4,2,16,128]{6,5,3,0,1,2,4:T(8,128)(2,1)S(1)}, u32[]{:S(2)}, u32[]{:S(2)}) collective-permute-start(bf16[2,2,2,4,2,16,128]{6,5,3,0,1,2,4:T(8,128)(2,1)S(1)} %fusion.9), channel_id=1, source_target_pairs={{0,1},{1,0},{2,3},{3,2},{4,5},{5,4},{6,7},{7,6},{8,9},{9,8},{10,11... | collective-permute-start | bytes 786440 | tf_op jit(solution)/shard_map/ppermute | solution.py:598
  184.2 19.9 %copy-start.17 = (bf16[512,512]{1,0:T(8,128)(2,1)S(1)}, bf16[512,512]{1,0:T(8,128)(2,1)}, u32[]{:S(2)}) copy-start(bf16[512,512]{1,0:T(8,128)(2,1)} %copy-done.16) | copy-start | bytes 1572868
  184.3 19.8 %copy-start.14 = (bf16[2,2,16,128,128]{4,3,2,1,0:T(8,128)(2,1)S(1)}, bf16[2,2,16,128,128]{4,3,2,1,0:T(8,128)(2,1)}, u32[]{:S(2)}) copy-start(bf16[2,2,16,128,128]{4,3,2,1,0:T(8,128)(2,1)} %copy-done.13) | copy-start | bytes 6291460
  184.3 19.8 %copy-start.15 = (bf16[16,16,16,256]{3,2,1,0:T(8,128)(2,1)S(1)}, bf16[16,16,16,256]{3,2,1,0:T(8,128)(2,1)}, u32[]{:S(2)}) copy-start(bf16[16,16,16,256]{3,2,1,0:T(8,128)(2,1)} %get-tuple-element.49.spec) | copy-start | bytes 6291460
  184.3 15.8 %collective-permute-start.1 = (bf16[2,2,2,8,16,128]{5,4,3,0,1,2:T(8,128)(2,1)S(1)}, bf16[2,2,2,8,16,128]{5,4,3,0,1,2:T(8,128)(2,1)S(1)}, u32[]{:S(2)}, u32[]{:S(2)}) collective-permute-start(bf16[2,2,2,8,16,128]{5,4,3,0,1,2:T(8,128)(2,1)S(1)} %fusion.8), channel_id=1, source_target_pairs={{0,2},{1,3},{2,0},{3,1},{4,6},{5,7},{6,4},{7,5},{8,10},{9,11},{10,... | collective-permute-start | bytes 786440 | tf_op jit(solution)/shard_map/ppermute | solution.py:598
  186.3 16.1 %collective-permute-start.3 = (bf16[2,2,2,4,16,128]{5,4,3,0,1,2:T(8,128)(2,1)S(1)}, bf16[2,2,2,4,16,128]{5,4,3,0,1,2:T(8,128)(2,1)S(1)}, u32[]{:S(2)}, u32[]{:S(2)}) collective-permute-start(bf16[2,2,2,4,16,128]{5,4,3,0,1,2:T(8,128)(2,1)S(1)} %fusion.11), channel_id=1, source_target_pairs={{0,2},{1,3},{2,0},{3,1},{4,6},{5,7},{6,4},{7,5},{8,10},{9,11},{10,... | collective-permute-start | bytes 393224 | tf_op jit(solution)/shard_map/ppermute | solution.py:598
  202.5 8.0 %collective-permute-start.4 = (bf16[2,2,12,16,128]{4,3,2,0,1:T(8,128)(2,1)S(1)}, bf16[2,2,12,16,128]{4,3,2,0,1:T(8,128)(2,1)S(1)}, u32[]{:S(2)}, u32[]{:S(2)}) collective-permute-start(bf16[2,2,12,16,128]{4,3,2,0,1:T(8,128)(2,1)S(1)} %fusion.10), channel_id=1, source_target_pairs={{0,4},{4,0},{8,12},{12,8},{16,20},{20,16},{24,28},{28,24},{1,5},{5... | collective-permute-start | bytes 589832 | tf_op jit(solution)/shard_map/ppermute | solution.py:598
  210.6 5.5 %collective-permute-start.5 = (bf16[2,12,16,128]{3,2,1,0:T(8,128)(2,1)S(1)}, bf16[2,12,16,128]{3,2,1,0:T(8,128)(2,1)S(1)}, u32[]{:S(2)}, u32[]{:S(2)}) collective-permute-start(bf16[2,12,16,128]{3,2,1,0:T(8,128)(2,1)S(1)} %fusion.12), channel_id=1, source_target_pairs={{0,8},{4,12},{8,0},{12,4},{16,24},{20,28},{24,16},{28,20},{1,9},{5... | collective-permute-start | bytes 294920 | tf_op jit(solution)/shard_map/ppermute | solution.py:598
  216.1 5.1 %collective-permute-start.6 = (bf16[12,16,128]{2,1,0:T(8,128)(2,1)S(1)}, bf16[12,16,128]{2,1,0:T(8,128)(2,1)S(1)}, u32[]{:S(2)}, u32[]{:S(2)}) collective-permute-start(bf16[12,16,128]{2,1,0:T(8,128)(2,1)S(1)} %fusion.17), channel_id=1, source_target_pairs={{0,16},{4,20},{8,24},{12,28},{16,0},{20,4},{24,8},{28,12},{1,17},{... | collective-permute-start | bytes 147464 | tf_op jit(solution)/shard_map/ppermute | solution.py:598
